TPU v7x, 128 devices: a whole 4x4x4 slice. The times are simulated.
128 devices in a mesh: pair: 32 (over z, y, x_lo), chol: 4 (over x_hi, core).
Axes of the slice: x: 4 (x_hi: 2, x_lo: 2; x = x_hi * 2 + x_lo), y: 4, z: 4, core: 2. Of those that a mesh axis runs over, the one named last changes fastest.
Arguments:
- left_vectors: bfloat16 [8, 160, 800], P(None, 'pair'), may hold values from -6 to 6
- chol_factors: bfloat16 [160, 800, 2560], P('pair', None, 'chol'), may hold values from -0.046875 to 0.046875
- eps_occ: float32 [160], P('pair'), may hold values from -1.5 to -0.3
- eps_vir: float32 [800], replicated, may hold values from 0.2 to 3
Outputs:
- left_sigma: float32 [8, 160, 800], P(None, 'pair')
All inputs are finite; a program needn't handle non-finite values.
Results may differ from a plain program's by a relative error of at most 0.0016.
Values may be sent and summed in bfloat16 or wider, within the bound.
No kernel may reach another device: no remote copies, remote signals or barrier semaphores. Data moves between devices by JAX's collectives and lax.ppermute only.
A program may use at most 64 MiB of HBM per device.

v0:
```python
import jax
import jax.numpy as jnp
from jax import lax
from jax.sharding import PartitionSpec as P


def body(left_vectors, chol_factors, eps_occ, eps_vir):
    occ_local = chol_factors.shape[0]
    gathered = lax.all_gather(left_vectors, "pair", axis=1, tiled=True)
    coul_part = jnp.einsum(
        "ria,iap->rp", left_vectors, chol_factors, preferred_element_type=jnp.float32
    )
    coul_vec = lax.psum(coul_part, "pair").astype(jnp.bfloat16)
    coulomb = jnp.einsum("iap,rp->ria", chol_factors, coul_vec, preferred_element_type=jnp.float32)
    z_local = jnp.einsum(
        "ibp,rjb->rijp", chol_factors, gathered, preferred_element_type=jnp.float32
    ).astype(jnp.bfloat16)
    exchange_term = jnp.einsum(
        "rijp,jap->ria",
        lax.all_to_all(z_local, "pair", split_axis=2, concat_axis=1, tiled=True),
        chol_factors,
        preferred_element_type=jnp.float32,
    )
    offset = lax.axis_index("pair") * occ_local
    partial_all = -exchange_term
    own_rows = lax.dynamic_slice_in_dim(partial_all, offset, occ_local, 1) + 2.0 * coulomb
    partial_all = lax.dynamic_update_slice_in_dim(partial_all, own_rows, offset, 1)
    summed_all = lax.psum(partial_all, ("pair", "chol"))
    summed = lax.dynamic_slice_in_dim(summed_all, offset, occ_local, 1)
    diagonal_part = (eps_vir[None, None, :] - eps_occ[None, :, None]) * left_vectors.astype(
        jnp.float32
    )
    return diagonal_part + summed


def solution(mesh):
    placed = (P(None, "pair", None), P("pair", None, "chol"), P("pair"), P())
    return jax.shard_map(
        body, mesh=mesh, in_specs=placed, out_specs=P(None, "pair", None), check_vma=False
    )
```

profile of v0, /device:TPU:1, one launch (start us, length us, event | category | flops | bytes accessed | tf_op | source)
XLA Modules:
  0.0 612.2 jit_solution(9357112869376586982)
XLA Ops:
  6.5 0.0 all-gather.2.cloned.1.call-start
  6.5 0.7 all-gather.2.cloned.1.call-update
  7.3 140.7 %all-gather.2.cloned.1.call-done = bf16[8,160,800]{2,0,1:T(8,128)(2,1)} async-done(((bf16[8,5,800]{2,0,1:T(8,128)(2,1)}), bf16[8,160,800]{2,0,1:T(8,128)(2,1)}) %all-gather.2.cloned.1.call-update) | async-done | bytes 2048016 | tf_op jit(solution)/shard_map/all_gather | solution.py:9
  147.9 11.9 %convert_bitcast_fusion = bf16[8,5,160,640]{3,2,1,0:T(8,128)(2,1)S(1)} fusion(bf16[5,800,640]{2,1,0:T(8,128)(2,1)} %param.5, bf16[8,160,800,1]{2,0,1,3:T(8,128)(2,1)} %bitcast.28), kind=kOutput, calls=%fused_computation | convolution fusion | flops 6557696000 | bytes 15360000 | tf_op jit(solution)/shard_map/ibp,rjb->rijp/dot_general | solution.py:15
  159.9 6.1 copy.34
  166.0 0.0 copy-start
  166.0 7.0 %all-to-all-start = ((bf16[8,5,160,640]{3,0,1,2:T(8,128)(2,1)}), bf16[8,5,160,640]{3,0,1,2:T(8,128)(2,1)}, u32[]{:S(2)}, u32[]{:S(2)}) async-start(bf16[8,5,160,640]{3,0,1,2:T(8,128)(2,1)} %copy.34), calls=%async_computation | async-start | bytes 16384000 | tf_op jit(solution)/shard_map/all_to_all | solution.py:20
  173.0 0.0 all-reduce.2.cloned.1.call-start
  173.0 0.0 copy-done
  173.0 0.0 slice-start
  173.1 3.3 convolution_bitcast_fusion
  176.4 206.2 %psum.14 = bf16[8,640]{1,0:T(8,128)(2,1)S(1)} all-reduce(f32[8,640]{1,0:T(8,128)S(1)} %convolution_bitcast_fusion), channel_id=1, replica_groups=mesh['pair'=32,'chol'=4] {'pair'}, use_global_device_ids=true, to_apply=%region_0.0 | all-reduce | flops 5120 | bytes 30720 | tf_op jit(solution)/shard_map/psum | solution.py:13
  382.6 0.0 all-to-all-done
  382.6 0.0 slice-start.1
  382.6 7.3 %copy.36 = bf16[8,32,5,5,640]{4,0,3,2,1:T(8,128)(2,1)} copy(bf16[8,32,5,5,640]{4,0,2,3,1:T(8,128)(2,1)} %bitcast.5) | data formatting | bytes 16384000 | tf_op jit(solution)/shard_map/all_to_all | solution.py:20
  389.9 0.0 slice-done
  390.0 0.0 slice-done.1
  390.0 12.7 %bitcast_negate_fusion = f32[8,160,800]{2,0,1:T(8,128)} fusion(bf16[8,160,5,640]{3,0,2,1:T(8,128)(2,1)} %bitcast.27, bf16[5,800,640]{2,1,0:T(8,128)(2,1)S(1)} %bitcast.26), kind=kOutput, calls=%fused_computation.4 | convolution fusion | flops 6554624000 | bytes 17408000 | tf_op jit(solution)/shard_map/rijp,jap->ria/dot_general | solution.py:18
  402.6 0.0 copy-start.1
  402.6 0.0 copy-start.2
  402.6 3.1 fusion.7
  405.7 0.0 all-reduce.2.cloned.1.call-update
  405.7 0.0 copy-done.1
  405.8 0.0 copy-done.2
  405.8 0.1 broadcast_subtract_fusion
  405.8 198.0 %all-reduce.2.cloned.1.call-done = f32[8,160,800]{2,0,1:T(8,128)} async-done(((f32[8,160,800]{2,0,1:T(8,128)}), f32[8,160,800]{2,0,1:T(8,128)}) %all-reduce.2.cloned.1.call-update) | async-done | bytes 4096016 | tf_op jit(solution)/shard_map/psum | solution.py:28
  603.8 1.6 dynamic-slice_add_fusion
  (1 shorter events, 0.0 us)
Async XLA Ops:
  6.5 141.4 %all-gather.2.cloned.1.call-start = ((), (), s32[]{:S(2)}) async-start(), calls=%async_computation.1 | async-start | bytes 2365440 | tf_op jit(solution)/shard_map/all_gather | solution.py:9
  166.0 7.1 %copy-start = (bf16[8,5,800]{2,0,1:T(8,128)(2,1)S(1)}, bf16[8,5,800]{2,0,1:T(8,128)(2,1)}, u32[]{:S(2)}) copy-start(bf16[8,5,800]{2,0,1:T(8,128)(2,1)} %param.4) | copy-start | bytes 192004
  166.0 216.6 %all-to-all-start = ((bf16[8,5,160,640]{3,0,1,2:T(8,128)(2,1)}), bf16[8,5,160,640]{3,0,1,2:T(8,128)(2,1)}, u32[]{:S(2)}, u32[]{:S(2)}) async-start(bf16[8,5,160,640]{3,0,1,2:T(8,128)(2,1)} %copy.34), calls=%async_computation | async-start | bytes 16384000 | tf_op jit(solution)/shard_map/all_to_all | solution.py:20
  173.0 430.8 %all-reduce.2.cloned.1.call-start = ((), (), s32[]{:S(2)}) async-start(), calls=%async_computation.2 | async-start | bytes 9175040 | tf_op jit(solution)/shard_map/psum | solution.py:28
  173.0 216.9 %slice-start = ((s8[5120000]{0:T(1024)(128)(4,1)}), s8[925696]{0:T(1024)(128)(4,1)S(1)}, s32[]{:S(2)}) async-start(s8[5120000]{0:T(1024)(128)(4,1)} %bitcast.25), calls=%async_computation.3 | async-start | bytes 1851392
  382.6 7.3 %slice-start.1 = ((s8[5120000]{0:T(1024)(128)(4,1)}), s8[4194304]{0:T(1024)(128)(4,1)S(1)}, s32[]{:S(2)}) async-start(s8[5120000]{0:T(1024)(128)(4,1)} %bitcast.25), calls=%async_computation.4 | async-start | bytes 8388608
  402.6 3.1 copy-start.1
  402.6 3.1 copy-start.2
Sparse Core Ops, SparseCore 0:
  9.0 138.8 all-gather.1
  405.9 197.8 all-reduce.1
where the time goes:
time: 612 us
  waiting for transfers between devices  339 us (55%)
  blocking collectives  206 us (34%)
  matrix products  31 us (5%)
  local copies, waits for them, and re-layouts  13.5 us (2%)
  between operations  13.5 us (2%)
  starting transfers between devices  7.04 us (1%)
    psum x1, blocking collectives, body(): coul_vec = lax.psum(coul_part, 'pair').astype(jnp.bfloat16)  206 us
    psum x1, waiting for transfers between devices, body(): summed_all = lax.psum(partial_all, ('pair', 'chol'))  198 us
    all_gather x1, waiting for transfers between devices, body(): gathered = lax.all_gather(left_vectors, 'pair', axis=1, tiled=True)  141 us
    dot_general x1, matrix products, body(): jnp.einsum('rijp,jap->ria', lax.all_to_all(z_local, 'pair', split_axis=2,...  12.7 us
  transfers between devices with their start and end apart: 3, of which 2 were waited for; matrix products, arithmetic and copies ran while one was open for 1% of the time, Pallas kernels for 0%

commit v1 on v0

v1 whole, which is shorter than its diff:
```python
import jax
import jax.numpy as jnp
from jax import lax
from jax.sharding import PartitionSpec as P

CORE_SWAP = [(0, 1), (1, 0), (2, 3), (3, 2)]
FAR_SWAP = [(0, 2), (2, 0), (1, 3), (3, 1)]


def exchange(blocks):
    return lax.all_to_all(blocks, "pair", split_axis=0, concat_axis=0, tiled=True)


def body(left_vectors, chol_factors, eps_occ, eps_vir):
    roots, occ_local, vir = left_vectors.shape
    aux_local = chol_factors.shape[2]
    ranks = lax.axis_size("pair")
    aux_own = aux_local // ranks
    occ = occ_local * ranks
    half = roots // 2
    core = lax.rem(lax.axis_index("chol"), 2)

    by_aux = chol_factors.reshape(occ_local * vir, aux_local).T
    by_aux = exchange(by_aux.reshape(ranks, aux_own, occ_local * vir))
    factors = by_aux.reshape(ranks, aux_own, occ_local, vir)

    own_half = lax.dynamic_slice_in_dim(left_vectors, core * half, half, 0)
    mine = exchange(jnp.broadcast_to(own_half[None], (ranks, half, occ_local, vir)))
    other = lax.ppermute(mine, "chol", CORE_SWAP)
    lefts = jnp.where(
        core == 0,
        jnp.concatenate([mine, other], axis=1),
        jnp.concatenate([other, mine], axis=1),
    )

    coul_part = jnp.einsum(
        "ria,iap->rp", left_vectors, chol_factors, preferred_element_type=jnp.float32
    )
    coul_part = exchange(coul_part.reshape(roots, ranks, aux_own).transpose(1, 0, 2))
    coul_own = jnp.sum(coul_part, axis=0).astype(jnp.bfloat16)
    coul_vec = exchange(jnp.broadcast_to(coul_own[None], (ranks, roots, aux_own)))
    coul_vec = coul_vec.transpose(1, 0, 2).reshape(roots, aux_local)
    coulomb = jnp.einsum("iap,rp->ria", chol_factors, coul_vec, preferred_element_type=jnp.float32)

    z_inter = jnp.einsum(
        "dpib,erjb->rdipej", factors, lefts, preferred_element_type=jnp.float32
    ).astype(jnp.bfloat16)
    partial_all = jnp.einsum(
        "rdipej,epja->dria", z_inter, factors, preferred_element_type=jnp.float32
    )

    keep = lax.dynamic_slice_in_dim(partial_all, core * half, half, 1)
    give = lax.dynamic_slice_in_dim(partial_all, (1 - core) * half, half, 1)
    keep = keep + lax.ppermute(give, "chol", CORE_SWAP)
    pieces = exchange(keep.astype(jnp.bfloat16))
    exch = jnp.sum(pieces.astype(jnp.float32), axis=0)

    coul_keep = lax.dynamic_slice_in_dim(coulomb, core * half, half, 0)
    coul_give = lax.dynamic_slice_in_dim(coulomb, (1 - core) * half, half, 0)
    coul_keep = coul_keep + lax.ppermute(coul_give, "chol", CORE_SWAP)
    part = 2.0 * coul_keep - exch
    part = part + lax.ppermute(part, "chol", FAR_SWAP)
    rest = lax.ppermute(part, "chol", CORE_SWAP)
    summed = jnp.where(
        core == 0,
        jnp.concatenate([part, rest], axis=0),
        jnp.concatenate([rest, part], axis=0),
    )
    diagonal_part = (eps_vir[None, None, :] - eps_occ[None, :, None]) * left_vectors.astype(
        jnp.float32
    )
    return diagonal_part + summed


def solution(mesh):
    placed = (P(None, "pair", None), P("pair", None, "chol"), P("pair"), P())
    return jax.shard_map(
        body, mesh=mesh, in_specs=placed, out_specs=P(None, "pair", None), check_vma=False
    )
```

time: 612 us -> 272 us (0.44)
  waiting for transfers between devices: 339 us -> 98.4 us
  blocking collectives: 206 us -> 21.2 us
  local copies, waits for them, and re-layouts: 13.5 us -> 46.7 us
  matrix products: 31 us -> 60.9 us
  starting transfers between devices: 7.04 us -> 36.7 us
  between operations: 13.5 us -> 0.16 us
    psum x1 -> x0, blocking collectives: 206 us -> none  [body(): coul_vec = lax.psum(coul_part, 'pair').astype(jnp.bfloat16)]
    psum x1 -> x0, waiting for transfers between devices: 198 us -> none  [body(): summed_all = lax.psum(partial_all, ('pair', 'chol'))]
    all_gather x1 -> x0, waiting for transfers between devices: 141 us -> none  [body(): gathered = lax.all_gather(left_vectors, 'pair', axis=1, tiled=True)]
    all_to_all x1 -> x4, waiting for transfers between devices: 0.01 us -> 92.9 us  [exchange(): lax.all_to_all(blocks, 'pair', split_axis=0, concat_axis=0, tiled=True)]
    dot_general x2, matrix products: 24.6 us -> 56.2 us  [the longest x1 39.3 us: body(): jnp.einsum('dpib,erjb->rdipej', factors, lefts, preferred_element_type=jn...]
    reshape x0 -> x5, local copies, waits for them, and re-layouts: none -> 29.4 us  [the longest x1 13.4 us: body(): factors = by_aux.reshape(ranks, aux_own, occ_local, vir)]
    all_to_all x0 -> x1, blocking collectives: none -> 21.2 us  [exchange(): lax.all_to_all(blocks, 'pair', split_axis=0, concat_axis=0, tiled=True)]
    all_to_all x1 -> x4, starting transfers between devices: 7 us -> 23.6 us  [exchange(): lax.all_to_all(blocks, 'pair', split_axis=0, concat_axis=0, tiled=True)]
  transfers between devices with their start and end apart: 3 -> 9, of which waited for: 2 -> 7; matrix products, arithmetic and copies ran while one was open for 1% -> 11% of each run, Pallas kernels for 0% -> 0%
where the time goes in v1:
time: 272 us; the launch traced here: 270 us
  waiting for transfers between devices  98.4 us (36%)
  matrix products  60.9 us (22%)
  local copies, waits for them, and re-layouts  46.7 us (17%)
  starting transfers between devices  36.7 us (13%)
  blocking collectives  21.2 us (8%)
  other arithmetic  6.19 us (2%)
    all_to_all x4, waiting for transfers between devices, exchange(): lax.all_to_all(blocks, 'pair', split_axis=0, concat_axis=0, tiled=True)  92.9 us
    dot_general x1, matrix products, body(): jnp.einsum('dpib,erjb->rdipej', factors, lefts, preferred_element_type=jn...  39.3 us
    all_to_all x4, starting transfers between devices, exchange(): lax.all_to_all(blocks, 'pair', split_axis=0, concat_axis=0, tiled=True)  23.6 us
    all_to_all x1, blocking collectives, exchange(): lax.all_to_all(blocks, 'pair', split_axis=0, concat_axis=0, tiled=True)  21.2 us
    dot_general x1, matrix products, body(): jnp.einsum('rdipej,epja->dria', z_inter, factors, preferred_element_type=...  16.8 us
    reshape x1, local copies, waits for them, and re-layouts, body(): factors = by_aux.reshape(ranks, aux_own, occ_local, vir)  13.4 us
    all_to_all x3, local copies, waits for them, and re-layouts, exchange(): lax.all_to_all(blocks, 'pair', split_axis=0, concat_axis=0, tiled=True)  8.6 us
    reshape x1, local copies, waits for them, and re-layouts, body(): by_aux = chol_factors.reshape(occ_local * vir, aux_local).T  7.92 us
  transfers between devices with their start and end apart: 9, of which 7 were waited for; matrix products, arithmetic and copies ran while one was open for 11% of the time, Pallas kernels for 0%

profile of v1, /device:TPU:1, one launch (start us, length us, event | category | flops | bytes accessed | tf_op | source)
XLA Modules:
  0.0 270.2 jit_solution(1406920280916159817)
XLA Ops:
  0.0 0.9 constant_dynamic-slice_fusion
  0.9 1.3 broadcast_in_dim.5
  2.2 9.8 %all-to-all-start.2 = ((bf16[32,4,5,800]{3,1,2,0:T(4,128)(2,1)}), bf16[32,4,5,800]{3,1,2,0:T(4,128)(2,1)S(1)}, u32[]{:S(2)}, u32[]{:S(2)}) async-start(bf16[32,4,5,800]{3,1,2,0:T(4,128)(2,1)} %broadcast_in_dim.5), calls=%async_computation.2 | async-start | bytes 2293760 | tf_op jit(solution)/shard_map/all_to_all | solution.py:11
  12.0 7.9 %copy.43 = bf16[4000,640]{0,1:T(8,128)(2,1)} copy(bf16[4000,640]{1,0:T(8,128)(2,1)} %bitcast.36) | data formatting | bytes 10240000 | tf_op jit(solution)/shard_map/reshape | solution.py:23
  20.0 7.8 %reshape.54 = bf16[32,20,4000]{2,1,0:T(8,128)(2,1)} reshape(bf16[640,4000]{1,0:T(8,128)(2,1)} %bitcast.39) | data formatting | bytes 10240000 | tf_op jit(solution)/shard_map/reshape | solution.py:24
  27.7 2.2 all-to-all-done.2
  29.9 5.7 %all-to-all-start.3 = ((bf16[32,20,4000]{2,1,0:T(8,128)(2,1)}), bf16[32,20,4000]{2,1,0:T(8,128)(2,1)}, u32[]{:S(2)}, u32[]{:S(2)}) async-start(bf16[32,20,4000]{2,1,0:T(8,128)(2,1)} %reshape.54), calls=%async_computation.3 | async-start | bytes 12582912 | tf_op jit(solution)/shard_map/all_to_all | solution.py:11
  35.6 0.1 copy.40
  35.7 1.6 collective-permute-start.1
  37.3 2.4 collective-permute-done.1
  39.7 0.6 copy.41
  40.3 2.3 fusion.8
  42.7 76.8 %all-to-all-done.3 = bf16[32,20,4000]{2,1,0:T(8,128)(2,1)} async-done(((bf16[32,20,4000]{2,1,0:T(8,128)(2,1)}), bf16[32,20,4000]{2,1,0:T(8,128)(2,1)}, u32[]{:S(2)}, u32[]{:S(2)}) %all-to-all-start.3) | async-done | bytes 5120032 | tf_op jit(solution)/shard_map/all_to_all | solution.py:11
  119.5 8.0 %copy.44 = bf16[32,20,4000]{2,0,1:T(8,128)(2,1)} copy(bf16[32,20,4000]{2,1,0:T(8,128)(2,1)} %all-to-all-done.3) | data formatting | bytes 10240000 | tf_op jit(solution)/shard_map/all_to_all | solution.py:11
  127.4 13.4 %reshape.55 = bf16[32,20,5,800]{3,2,0,1:T(8,128)(2,1)} reshape(bf16[32,20,4000]{2,0,1:T(8,128)(2,1)} %copy.44) | data formatting | bytes 10240000 | tf_op jit(solution)/shard_map/reshape | solution.py:25
  140.9 39.3 %fusion.36 = bf16[8,32,5,20,32,5]{1,4,3,5,2,0:T(8,128)(2,1)} fusion(bf16[32,20,5,800,1,1]{3,2,0,1,5,4:T(8,128)(2,1)} %bitcast.40, bf16[32,8,5,800,1,1]{3,1,2,0,5,4:T(8,128)(2,1)S(1)} %fusion.8), kind=kOutput, calls=%fused_computation.1.clone.clone.clone.1 | convolution fusion | flops 6557696000 | bytes 15360000 | tf_op jit(solution)/shard_map/dpib,erjb->rdipej/dot_general | solution.py:45
  180.2 0.0 copy-done
  180.2 16.8 %fusion.12 = f32[8,32,5,800]{3,1,2,0:T(8,128)} fusion(bf16[32,20,5,800,1,1]{3,2,0,1,5,4:T(8,128)(2,1)S(1)} %bitcast.41, bf16[8,32,5,20,32,5]{1,4,3,5,2,0:T(8,128)(2,1)} %fusion.36), kind=kOutput, calls=%fused_computation.13 | convolution fusion | flops 6553600000 | bytes 17408000 | tf_op jit(solution)/shard_map/rdipej,epja->dria/dot_general | solution.py:48
  197.0 3.2 %dynamic-slice_bitcast_fusion = f32[32,4,5,800]{3,0,2,1:T(8,128)} fusion(f32[8,32,5,800]{3,1,2,0:T(8,128)} %fusion.12, s32[]{:T(128)S(6)} %select_n.27), kind=kLoop, calls=%fused_computation.12 | loop fusion | bytes 4096004 | tf_op jit(solution)/shard_map/dynamic_slice | solution.py:53
  200.3 2.3 collective-permute-start.2
  202.6 0.0 copy-done.1
  202.6 0.8 convolution_bitcast_fusion
  203.4 0.2 reshape.51
  203.5 0.1 copy.38
  203.6 0.1 reshape.63
  203.8 21.2 %all_to_all.25 = f32[32,1,160]{2,1,0:T(1,128)S(1)} all-to-all(f32[32,1,160]{2,1,0:T(1,128)S(1)} %reshape.63), channel_id=1, replica_groups=mesh['pair'=32,'chol'=4] {'pair'}, dimensions={0} | all-to-all | bytes 40960 | tf_op jit(solution)/shard_map/all_to_all | solution.py:11
  225.0 0.5 broadcast.26
  225.5 0.7 reduce
  226.3 0.1 reshape.64
  226.4 0.6 broadcast_in_dim.4
  227.0 3.9 %all-to-all-start.1 = ((bf16[32,8,20]{2,1,0:T(8,128)(2,1)}), bf16[32,8,20]{2,1,0:T(8,128)(2,1)S(1)}, u32[]{:S(2)}, u32[]{:S(2)}) async-start(bf16[32,8,20]{2,1,0:T(8,128)(2,1)} %broadcast_in_dim.4), calls=%async_computation.1 | async-start | bytes 131072 | tf_op jit(solution)/shard_map/all_to_all | solution.py:11
  230.9 0.0 collective-permute-done.2
  230.9 2.0 fusion.9
  232.9 1.6 copy.49
  234.5 3.6 %all-to-all-done.1 = bf16[32,8,20]{2,1,0:T(8,128)(2,1)S(1)} async-done(((bf16[32,8,20]{2,1,0:T(8,128)(2,1)}), bf16[32,8,20]{2,1,0:T(8,128)(2,1)S(1)}, u32[]{:S(2)}, u32[]{:S(2)}) %all-to-all-start.1) | async-done | bytes 10272 | tf_op jit(solution)/shard_map/all_to_all | solution.py:11
  238.1 4.3 %all-to-all-start.4 = ((bf16[32,4,5,800]{3,1,2,0:T(4,128)(2,1)}), bf16[32,4,5,800]{3,1,2,0:T(4,128)(2,1)S(1)}, u32[]{:S(2)}, u32[]{:S(2)}) async-start(bf16[32,4,5,800]{3,1,2,0:T(4,128)(2,1)} %copy.49), calls=%async_computation.4 | async-start | bytes 2293760 | tf_op jit(solution)/shard_map/all_to_all | solution.py:11
  242.4 0.1 reshape.57
  242.5 4.0 %fusion.22 = f32[8,5,800]{2,0,1:T(8,128)S(1)} fusion(bf16[8,640,1]{1,0,2:T(8,128)(2,1)S(1)} %reshape.57, bf16[5,800,640]{2,1,0:T(8,128)(2,1)} %param.5), kind=kOutput, calls=%fused_computation.21 | convolution fusion | flops 40960000 | bytes 5258240 | tf_op jit(solution)/shard_map/iap,rp->ria/dot_general | solution.py:43
  246.5 2.2 collective-permute-start
  248.7 10.3 %all-to-all-done.4 = bf16[32,4,5,800]{3,1,2,0:T(4,128)(2,1)S(1)} async-done(((bf16[32,4,5,800]{3,1,2,0:T(4,128)(2,1)}), bf16[32,4,5,800]{3,1,2,0:T(4,128)(2,1)S(1)}, u32[]{:S(2)}, u32[]{:S(2)}) %all-to-all-start.4) | async-done | bytes 1024032 | tf_op jit(solution)/shard_map/all_to_all | solution.py:11
  259.1 0.2 convert_reduce_fusion
  259.3 0.0 collective-permute-done
  259.4 2.5 collective-permute-start.3
  261.9 2.2 collective-permute-done.3
  264.1 4.5 %collective-permute-start.4 = (f32[4,5,800]{2,0,1:T(4,128)S(1)}, f32[4,5,800]{2,0,1:T(4,128)S(1)}, u32[]{:S(2)}, u32[]{:S(2)}) collective-permute-start(f32[4,5,800]{2,0,1:T(4,128)S(1)} %add.25), channel_id=1, source_target_pairs={{0,1},{1,0},{2,3},{3,2},{4,5},{5,4},{6,7},{7,6},{8,9},{9,8},{10,11... | collective-permute-start | bytes 192008 | tf_op jit(solution)/shard_map/ppermute | solution.py:63
  268.6 0.1 broadcast_subtract_fusion
  268.7 0.8 collective-permute-done.4
  269.5 0.7 fusion.21
  (16 shorter events, 0.2 us)
Async XLA Ops:
  2.2 27.6 %all-to-all-start.2 = ((bf16[32,4,5,800]{3,1,2,0:T(4,128)(2,1)}), bf16[32,4,5,800]{3,1,2,0:T(4,128)(2,1)S(1)}, u32[]{:S(2)}, u32[]{:S(2)}) async-start(bf16[32,4,5,800]{3,1,2,0:T(4,128)(2,1)} %broadcast_in_dim.5), calls=%async_computation.2 | async-start | bytes 2293760 | tf_op jit(solution)/shard_map/all_to_all | solution.py:11
  29.9 89.6 %all-to-all-start.3 = ((bf16[32,20,4000]{2,1,0:T(8,128)(2,1)}), bf16[32,20,4000]{2,1,0:T(8,128)(2,1)}, u32[]{:S(2)}, u32[]{:S(2)}) async-start(bf16[32,20,4000]{2,1,0:T(8,128)(2,1)} %reshape.54), calls=%async_computation.3 | async-start | bytes 12582912 | tf_op jit(solution)/shard_map/all_to_all | solution.py:11
  35.7 4.0 %collective-permute-start.1 = (bf16[32,4,5,800]{3,0,2,1:T(8,128)(2,1)S(1)}, bf16[32,4,5,800]{3,0,2,1:T(8,128)(2,1)S(1)}, u32[]{:S(2)}, u32[]{:S(2)}) collective-permute-start(bf16[32,4,5,800]{3,0,2,1:T(8,128)(2,1)S(1)} %copy.40), channel_id=1, source_target_pairs={{0,1},{1,0},{2,3},{3,2},{4,5},{5,4},{6,7},{7,6},{8,9},{9,8},{10,11... | collective-permute-start | bytes 3072008 | tf_op jit(solution)/shard_map/ppermute | solution.py:29
  127.4 75.2 %slice-start = ((s8[5120000]{0:T(1024)(128)(4,1)}), s8[925696]{0:T(1024)(128)(4,1)S(1)}, s32[]{:S(2)}) async-start(s8[5120000]{0:T(1024)(128)(4,1)} %bitcast.37), calls=%async_computation.5 | async-start | bytes 1851392
  140.9 39.4 %copy-start = (bf16[32,20,5,800]{3,2,0,1:T(8,128)(2,1)S(1)}, bf16[32,20,5,800]{3,2,0,1:T(8,128)(2,1)}, u32[]{:S(2)}) copy-start(bf16[32,20,5,800]{3,2,0,1:T(8,128)(2,1)} %reshape.55) | copy-start | bytes 15360004
  140.9 61.7 %slice-start.1 = ((s8[5120000]{0:T(1024)(128)(4,1)}), s8[4194304]{0:T(1024)(128)(4,1)S(1)}, s32[]{:S(2)}) async-start(s8[5120000]{0:T(1024)(128)(4,1)} %bitcast.37), calls=%async_computation.6 | async-start | bytes 8388608
  197.0 5.6 %copy-start.1 = (bf16[8,5,800]{2,0,1:T(8,128)(2,1)S(1)}, bf16[8,5,800]{2,0,1:T(8,128)(2,1)}, u32[]{:S(2)}) copy-start(bf16[8,5,800]{2,0,1:T(8,128)(2,1)} %param.4) | copy-start | bytes 192004
  200.3 30.7 %collective-permute-start.2 = (f32[32,4,5,800]{3,0,2,1:T(8,128)}, f32[32,4,5,800]{3,0,2,1:T(8,128)S(1)}, u32[]{:S(2)}, u32[]{:S(2)}) collective-permute-start(f32[32,4,5,800]{3,0,2,1:T(8,128)} %dynamic-slice_bitcast_fusion), channel_id=1, source_target_pairs={{0,1},{1,0},{2,3},{3,2},{4,5},{5,4},{6,7},{7,6},{8,9},{9,8},{10,11... | collective-permute-start | bytes 6144008 | tf_op jit(solution)/shard_map/ppermute | solution.py:54
  227.0 11.1 %all-to-all-start.1 = ((bf16[32,8,20]{2,1,0:T(8,128)(2,1)}), bf16[32,8,20]{2,1,0:T(8,128)(2,1)S(1)}, u32[]{:S(2)}, u32[]{:S(2)}) async-start(bf16[32,8,20]{2,1,0:T(8,128)(2,1)} %broadcast_in_dim.4), calls=%async_computation.1 | async-start | bytes 131072 | tf_op jit(solution)/shard_map/all_to_all | solution.py:11
  234.5 34.1 %copy-start.2 = (f32[800]{0:T(1024)S(1)}, f32[800]{0:T(1024)}, u32[]{:S(2)}) copy-start(f32[800]{0:T(1024)} %param.7) | copy-start | bytes 9604
  234.5 34.1 %copy-start.3 = (f32[5]{0:T(128)S(1)}, f32[5]{0:T(128)}, u32[]{:S(2)}) copy-start(f32[5]{0:T(128)} %param.6) | copy-start | bytes 64
  238.1 20.9 %all-to-all-start.4 = ((bf16[32,4,5,800]{3,1,2,0:T(4,128)(2,1)}), bf16[32,4,5,800]{3,1,2,0:T(4,128)(2,1)S(1)}, u32[]{:S(2)}, u32[]{:S(2)}) async-start(bf16[32,4,5,800]{3,1,2,0:T(4,128)(2,1)} %copy.49), calls=%async_computation.4 | async-start | bytes 2293760 | tf_op jit(solution)/shard_map/all_to_all | solution.py:11
  246.5 12.8 %collective-permute-start = (f32[4,5,800]{2,0,1:T(4,128)S(1)}, f32[4,5,800]{2,0,1:T(4,128)S(1)}, u32[]{:S(2)}, u32[]{:S(2)}) collective-permute-start(f32[4,5,800]{2,0,1:T(4,128)S(1)} %constant_dynamic-slice_fusion.1), channel_id=1, source_target_pairs={{0,1},{1,0},{2,3},{3,2},{4,5},{5,4},{6,7},{7,6},{8,9},{9,8},{10,11... | collective-permute-start | bytes 192008 | tf_op jit(solution)/shard_map/ppermute | solution.py:60
  259.4 4.8 %collective-permute-start.3 = (f32[4,5,800]{2,0,1:T(4,128)S(1)}, f32[4,5,800]{2,0,1:T(4,128)S(1)}, u32[]{:S(2)}, u32[]{:S(2)}) collective-permute-start(f32[4,5,800]{2,0,1:T(4,128)S(1)} %copy_subtract_fusion), channel_id=1, source_target_pairs={{0,2},{2,0},{1,3},{3,1},{4,6},{6,4},{5,7},{7,5},{8,10},{10,8},{9,1... | collective-permute-start | bytes 192008 | tf_op jit(solution)/shard_map/ppermute | solution.py:62
  264.1 5.4 %collective-permute-start.4 = (f32[4,5,800]{2,0,1:T(4,128)S(1)}, f32[4,5,800]{2,0,1:T(4,128)S(1)}, u32[]{:S(2)}, u32[]{:S(2)}) collective-permute-start(f32[4,5,800]{2,0,1:T(4,128)S(1)} %add.25), channel_id=1, source_target_pairs={{0,1},{1,0},{2,3},{3,2},{4,5},{5,4},{6,7},{7,6},{8,9},{9,8},{10,11... | collective-permute-start | bytes 192008 | tf_op jit(solution)/shard_map/ppermute | solution.py:63

commit v2 on v0

v2 whole, which is shorter than its diff:
```python
import functools

import jax
import jax.numpy as jnp
from jax import lax
from jax.experimental import pallas as pl
from jax.experimental.pallas import tpu as pltpu
from jax.sharding import PartitionSpec as P

CORE_SWAP = [(0, 1), (1, 0), (2, 3), (3, 2)]
FAR_SWAP = [(0, 2), (2, 0), (1, 3), (3, 1)]
LANES = 128
FIRST = 12
CHUNK = 1024
VMEM = pl.BlockSpec(memory_space=pltpu.VMEM)
HIGH = 48 * 1024 * 1024
NT = (((1,), (1,)), ((), ()))


def exchange(blocks):
    return lax.all_to_all(blocks, "pair", split_axis=0, concat_axis=0, tiled=True)


def up(value, unit):
    return pl.cdiv(value, unit) * unit


def iota(shape, axis):
    return lax.broadcasted_iota(jnp.int32, shape, axis)


def one_hot(flag):
    return jnp.where(flag, 1.0, 0.0).astype(jnp.bfloat16)


def dot(a, b):
    return jnp.dot(a, b, preferred_element_type=jnp.float32)


def pack_kernel(dims, factors_ref, left_ref, first_ref, second_ref, sums):
    ranks, share, rows, roots = dims
    half = roots // 2
    rest = share - FIRST
    pitch = FIRST + half
    cut = ranks * FIRST
    aux = ranks * share
    k = pl.program_id(0)
    last = pl.cdiv(rows, CHUNK) - 1

    row, col = iota((ranks * pitch, cut), 0), iota((ranks * pitch, cut), 1)
    pick = one_hot((row % pitch < FIRST) & (col == row // pitch * FIRST + row % pitch))
    row, col = iota((ranks * pitch, roots), 0), iota((ranks * pitch, roots), 1)
    lay = one_hot(row % pitch == FIRST + col)
    keep = one_hot(iota((aux - cut, aux - cut), 0) == iota((aux - cut, aux - cut), 1))

    def some(size):
        block = factors_ref[:size, :]
        left = left_ref[:, :size]
        moved = lax.dot_general(pick, block[:, :cut], NT, preferred_element_type=jnp.float32)
        first_ref[:, :size] = (moved + dot(lay, left)).astype(jnp.bfloat16)
        moved = lax.dot_general(keep, block[:, cut:], NT, preferred_element_type=jnp.float32)
        second_ref[:, :size] = moved.astype(jnp.bfloat16)
        return dot(left, block)

    @pl.when(k == 0)
    def _():
        sums[...] = some(CHUNK)

    @pl.when((k > 0) & (k < last))
    def _():
        sums[...] += some(CHUNK)

    @pl.when(k == last)
    def _():
        size = rows - last * CHUNK
        left_over = sums[...] + some(size)
        row, col = iota((ranks * pitch, roots), 0), iota((ranks * pitch, roots), 1)
        lay_root = one_hot(row % pitch == col)
        row, col = iota((ranks * pitch, aux), 0), iota((ranks * pitch, aux), 1)
        owner = jnp.where(col < cut, col // FIRST, (col - cut) // rest)
        mine = owner == row // pitch
        spare = CHUNK - size
        row, col = iota((aux, spare), 0), iota((aux, spare), 1)
        slot = jnp.where(row < cut, row % FIRST, FIRST + (row - cut) % rest)
        extra = jnp.zeros((ranks * pitch, spare), jnp.float32)
        for t in range(3):
            term = left_over.astype(jnp.bfloat16)
            left_over = left_over - term.astype(jnp.float32)
            spread = jnp.where(mine, dot(lay_root, term), 0.0).astype(jnp.bfloat16)
            extra = extra + dot(spread, one_hot(col == t * share + slot))
        first_ref[:, size:] = extra.astype(jnp.bfloat16)
        second_ref[:, size:] = jnp.zeros((ranks * rest, spare), jnp.bfloat16)


def pack(factors, lefts, dims):
    ranks, share, rows, roots = dims
    pitch = FIRST + roots // 2
    rest = share - FIRST
    steps = pl.cdiv(rows, CHUNK)
    return pl.pallas_call(
        functools.partial(pack_kernel, dims),
        grid=(steps,),
        in_specs=[
            pl.BlockSpec((CHUNK, ranks * share), lambda k: (k, 0)),
            pl.BlockSpec((roots, CHUNK), lambda k: (0, k)),
        ],
        out_specs=[
            pl.BlockSpec((ranks * pitch, CHUNK), lambda k: (0, k)),
            pl.BlockSpec((ranks * rest, CHUNK), lambda k: (0, k)),
        ],
        out_shape=[
            jax.ShapeDtypeStruct((ranks * pitch, steps * CHUNK), jnp.bfloat16),
            jax.ShapeDtypeStruct((ranks * rest, steps * CHUNK), jnp.bfloat16),
        ],
        scratch_shapes=[pltpu.VMEM((roots, ranks * share), jnp.float32)],
        compiler_params=pltpu.CompilerParams(vmem_limit_bytes=HIGH),
    )(factors, lefts)


def coul_kernel(dims, got_ref, send_ref, out_ref):
    ranks, share, rows, roots = dims
    pitch = FIRST + roots // 2
    rest = share - FIRST
    start = rows % LANES
    row, col = iota((roots, ranks * pitch), 0), iota((roots, ranks * pitch), 1)
    sums = dot(one_hot(col % pitch == row), got_ref[...])
    turn = LANES - share
    once = pltpu.roll(sums, turn, 1)
    sums = sums + once + pltpu.roll(once, turn, 1)
    row, col = iota((ranks * rest, roots), 0), iota((ranks * rest, roots), 1)
    laid = dot(one_hot(row % rest == col), sums.astype(jnp.bfloat16)).astype(jnp.bfloat16)
    lane = iota((ranks * rest, LANES), 1)
    out_ref[...] = jnp.where(lane < start, send_ref[...], laid)


def coul_round(got, send, dims):
    ranks, share, rows, roots = dims
    at = rows // LANES
    return pl.pallas_call(
        functools.partial(coul_kernel, dims),
        grid=(1,),
        in_specs=[
            pl.BlockSpec((got.shape[0], LANES), lambda k: (0, at)),
            pl.BlockSpec((send.shape[0], LANES), lambda k: (0, at)),
        ],
        out_specs=pl.BlockSpec((send.shape[0], LANES), lambda k: (0, at)),
        out_shape=jax.ShapeDtypeStruct(send.shape, send.dtype),
        input_output_aliases={1: 0},
    )(got, send)


def left_kernel(dims, got_ref, out_ref):
    ranks, occ_local, vir, half = dims
    pitch = FIRST + half
    main = ranks * (occ_local - 1)
    for r in range(half):
        row, col = iota((ranks, ranks * pitch), 0), iota((ranks, ranks * pitch), 1)
        turn = one_hot(col == row * pitch + FIRST + r)
        for i in range(occ_local):
            part = dot(turn, got_ref[:, i * vir : (i + 1) * vir]).T.astype(jnp.bfloat16)
            to = r * main + i * ranks if i < occ_local - 1 else half * main + r * ranks
            out_ref[:, to : to + ranks] = part


def left_half(got, dims):
    ranks, occ_local, vir, half = dims
    return pl.pallas_call(
        functools.partial(left_kernel, dims),
        in_specs=[VMEM],
        out_specs=VMEM,
        out_shape=jax.ShapeDtypeStruct((vir, half * ranks * occ_local), jnp.bfloat16),
        compiler_params=pltpu.CompilerParams(vmem_limit_bytes=24 * 1024 * 1024),
    )(got)


def slab_kernel(dims, final, recv_ref, mine_ref, other_ref, *refs):
    ranks, share, pitch, occ_local, vir, roots = dims
    if final:
        total_ref, keep_ref, give_ref, left, rows_z, rows_e, zed = refs
    else:
        out_ref, left, rows_z, rows_e, zed = refs
    occ = ranks * occ_local
    main = occ - ranks
    packed = main // ranks
    half = roots // 2

    @pl.when(pl.program_id(0) == 0)
    def _():
        for h, ref in enumerate((mine_ref, other_ref)):
            left[:, h * half * main : (h + 1) * half * main] = ref[:, : half * main]
            to = roots * main + h * half * ranks
            left[:, to : to + half * ranks] = ref[:, half * main :]

        group = min(ranks, 256 // pitch)
        row, col = iota((group * share, group * pitch), 0), iota((group * share, group * pitch), 1)
        turn = one_hot(col == (row % group) * pitch + row // group)
        for at in range(ranks // group):
            for i in range(occ_local):
                part = recv_ref[
                    at * group * pitch : (at + 1) * group * pitch, i * vir : (i + 1) * vir
                ]
                part = dot(turn, part).astype(jnp.bfloat16)
                for s in range(share):
                    rows = part[s * group : (s + 1) * group]
                    to = s * occ + i * ranks + at * group
                    rows_z[to : to + group, :] = rows
                    if i < occ_local - 1:
                        to = s * main + i * ranks + at * group
                    else:
                        to = share * main + s * ranks + at * group
                    rows_e[to : to + group, :] = rows

        place = iota((occ, main), 1) // ranks

        def some_vectors(k, carry):
            at = pl.multiple_of(k * packed * occ, packed * occ)
            z = dot(rows_z[pl.ds(at, packed * occ), :], left[...]).astype(jnp.bfloat16)
            for r in range(roots):
                low = roots * main + (r // packed) * main
                rest = jnp.zeros((occ, main), jnp.bfloat16)
                for s in range(packed):
                    zs = z[s * occ : (s + 1) * occ]
                    to = pl.multiple_of(k * packed * main, packed * main) + s * main
                    zed[r * occ : (r + 1) * occ, pl.ds(to, main)] = zs[:, r * main : (r + 1) * main]
                    turned = zs[:, low : low + main]
                    shift = (s - r % packed) % packed * ranks
                    if shift:
                        turned = pltpu.roll(turned, shift, 1)
                    rest = jnp.where(place == s, turned, rest)
                to = pl.multiple_of(share * main + k * main, main)
                zed[r * occ : (r + 1) * occ, pl.ds(to, main)] = rest
            return carry

        lax.fori_loop(0, share // packed, some_vectors, 0)

    if not final:
        step = out_ref.shape[0]
        at = pl.multiple_of(pl.program_id(0) * step, step)
        out_ref[:, :vir] = dot(zed[pl.ds(at, step), :], rows_e[...])
        return
    step = half * occ

    @pl.when(pl.program_id(0) == 0)
    def _():
        keep_ref[:, :vir] = total_ref[:, :vir] + dot(zed[:step, :], rows_e[...])

    @pl.when(pl.program_id(0) == 1)
    def _():
        give_ref[:, :vir] = total_ref[:, :vir] + dot(zed[step:, :], rows_e[...])


def slab_product(recv, mine, other, total, dims):
    ranks, share, pitch, occ_local, vir, roots = dims
    occ = ranks * occ_local
    width = up(vir, LANES)
    final = total is not None
    steps = 2 if final else 4
    rows = roots * occ // steps
    args = [recv, mine, other] + ([total] if final else [])
    block = pl.BlockSpec((rows, width), lambda k: (k, 0))
    fixed = pl.BlockSpec((rows, width), lambda k: (0, 0))
    shape = jax.ShapeDtypeStruct((rows if final else roots * occ, width), jnp.float32)
    return pl.pallas_call(
        functools.partial(slab_kernel, dims, final),
        grid=(steps,),
        in_specs=[VMEM, VMEM, VMEM] + ([block] if final else []),
        out_specs=[fixed, fixed] if final else block,
        out_shape=[shape, shape] if final else shape,
        scratch_shapes=[
            pltpu.VMEM((vir, roots * occ), jnp.bfloat16),
            pltpu.VMEM((share * occ, vir), jnp.bfloat16),
            pltpu.VMEM((share * occ, vir), jnp.bfloat16),
            pltpu.VMEM((roots * occ, share * occ), jnp.bfloat16),
        ],
        compiler_params=pltpu.CompilerParams(vmem_limit_bytes=HIGH),
        cost_estimate=pl.CostEstimate(
            flops=4 * share * occ * roots * occ * vir,
            transcendentals=0,
            bytes_accessed=2 * share * occ * vir + 8 * roots * occ * vir,
        ),
    )(*args)


def merge_kernel(keep_ref, other_ref, out_ref, tiles):
    ranks, occ_local, half, vir = out_ref.shape
    occ = ranks * occ_local
    for t in range(tiles.shape[0]):
        at = slice(t * LANES, (t + 1) * LANES)
        tiles[t] = keep_ref[:, at] + other_ref[:, at]
    for d in range(ranks):
        for i in range(occ_local):
            for t in range(tiles.shape[0]):
                at = t * LANES
                size = min(LANES, vir - at)
                rows = tiles[t, pl.ds(i * ranks + d, half, stride=occ), :]
                out_ref[d, i, :, at : at + size] = rows[:, :size].astype(jnp.bfloat16)


def merge(keep, other, shape):
    rows, width = keep.shape
    return pl.pallas_call(
        merge_kernel,
        in_specs=[VMEM, VMEM],
        out_specs=VMEM,
        out_shape=jax.ShapeDtypeStruct(shape, jnp.bfloat16),
        scratch_shapes=[pltpu.VMEM((width // LANES, rows, LANES), jnp.float32)],
        compiler_params=pltpu.CompilerParams(vmem_limit_bytes=24 * 1024 * 1024),
    )(keep, other)


def body(left_vectors, chol_factors, eps_occ, eps_vir):
    roots, occ_local, vir = left_vectors.shape
    aux_local = chol_factors.shape[2]
    ranks = lax.axis_size("pair")
    share = aux_local // ranks
    rest = share - FIRST
    rows = occ_local * vir
    occ = occ_local * ranks
    half = roots // 2
    core = lax.rem(lax.axis_index("chol"), 2)
    dims = (ranks, share, rows, roots)

    turned = jnp.where(
        core == 0, left_vectors, jnp.concatenate([left_vectors[half:], left_vectors[:half]], axis=0)
    )
    flat = turned.reshape(roots, rows)
    first_send, second_send = pack(
        chol_factors.reshape(rows, aux_local),
        jnp.pad(flat, ((0, 0), (0, up(rows, CHUNK) - rows))),
        dims,
    )

    pitch = FIRST + half
    first = exchange(first_send.reshape(ranks, pitch, -1)).reshape(ranks * pitch, -1)
    second_send = coul_round(first, second_send, dims)
    second = exchange(second_send.reshape(ranks, rest, -1)).reshape(ranks * rest, -1)
    mine = left_half(first, (ranks, occ_local, vir, half))
    other = lax.ppermute(mine, "chol", CORE_SWAP)

    total = slab_product(first, mine, other, None, (ranks, FIRST, pitch, occ_local, vir, roots))
    keep, give = slab_product(
        second, mine, other, total, (ranks, rest, rest, occ_local, vir, roots)
    )

    merged = merge(keep, lax.ppermute(give, "chol", CORE_SWAP), (ranks, occ_local, half, vir))
    merged, second = lax.optimization_barrier((merged, second))
    pieces = exchange(merged)
    exch = jnp.sum(pieces.astype(jnp.float32), axis=0).transpose(1, 0, 2)

    coul_vec = second[:, rows : rows + share].reshape(ranks, roots, share).transpose(1, 0, 2)
    coul_vec = jnp.concatenate(
        [
            coul_vec[:, :, :FIRST].reshape(roots, ranks * FIRST),
            coul_vec[:, :, FIRST:].reshape(roots, ranks * rest),
        ],
        axis=1,
    )
    coulomb = jnp.einsum("iap,rp->ria", chol_factors, coul_vec, preferred_element_type=jnp.float32)
    coul_keep = coulomb[:half] + lax.ppermute(coulomb[half:], "chol", CORE_SWAP)

    part = 2.0 * coul_keep - exch
    part = part + lax.ppermute(part, "chol", FAR_SWAP)
    rest_part = lax.ppermute(part, "chol", CORE_SWAP)
    summed = jnp.where(
        core == 0,
        jnp.concatenate([part, rest_part], axis=0),
        jnp.concatenate([rest_part, part], axis=0),
    )
    diagonal_part = (eps_vir[None, None, :] - eps_occ[None, :, None]) * left_vectors.astype(
        jnp.float32
    )
    return diagonal_part + summed


def solution(mesh):
    placed = (P(None, "pair", None), P("pair", None, "chol"), P("pair"), P())
    return jax.shard_map(
        body, mesh=mesh, in_specs=placed, out_specs=P(None, "pair", None), check_vma=False
    )
```

time: 612 us -> 172 us (0.28)
  waiting for transfers between devices: 339 us -> 22.4 us
  blocking collectives: 206 us -> 59.5 us
  Pallas kernels: 0 us -> 54.6 us
  matrix products: 31 us -> 3.99 us
  starting transfers between devices: 7.04 us -> 21.9 us
  between operations: 13.5 us -> 0.13 us
    psum x1 -> x0, blocking collectives: 206 us -> none  [body(): coul_vec = lax.psum(coul_part, 'pair').astype(jnp.bfloat16)]
    psum x1 -> x0, waiting for transfers between devices: 198 us -> none  [body(): summed_all = lax.psum(partial_all, ('pair', 'chol'))]
    all_gather x1 -> x0, waiting for transfers between devices: 141 us -> none  [body(): gathered = lax.all_gather(left_vectors, 'pair', axis=1, tiled=True)]
    all_to_all x0 -> x1, blocking collectives: none -> 59.5 us  [exchange(): lax.all_to_all(blocks, 'pair', split_axis=0, concat_axis=0, tiled=True)]
    pallas_call x0 -> x6, Pallas kernels: none -> 54.6 us  [the longest x2 30.6 us: slab_product(): pl.pallas_call(functools.partial(slab_kernel, dims, final), grid=(steps,)...]
    dot_general x3 -> x0, matrix products: 27.9 us -> none  [the longest x1 12.7 us: body(): jnp.einsum('rijp,jap->ria', lax.all_to_all(z_local, 'pair', split_axis=2,...]
    all_to_all x1 -> x2, waiting for transfers between devices: 0.01 us -> 12.8 us  [exchange(): lax.all_to_all(blocks, 'pair', split_axis=0, concat_axis=0, tiled=True)]
    ppermute x0 -> x5, waiting for transfers between devices: none -> 9.61 us  [the longest x1 4.28 us: body(): lax.ppermute(give, 'chol', CORE_SWAP)]
  transfers between devices with their start and end apart: 3 -> 7, of which waited for: 2 -> 5; matrix products, arithmetic and copies ran while one was open for 1% -> 3% of each run, Pallas kernels for 0% -> 15%
where the time goes in v2:
time: 172 us
  blocking collectives  59.5 us (35%)
  Pallas kernels  54.6 us (32%)
  waiting for transfers between devices  22.4 us (13%)
  starting transfers between devices  21.9 us (13%)
  local copies, waits for them, and re-layouts  7.68 us (4%)
  matrix products  3.99 us (2%)
    all_to_all x1, blocking collectives, exchange(): lax.all_to_all(blocks, 'pair', split_axis=0, concat_axis=0, tiled=True)  59.5 us
    pallas_call x2, Pallas kernels, slab_product(): pl.pallas_call(functools.partial(slab_kernel, dims, final), grid=(steps,)...  30.6 us
    all_to_all x2, waiting for transfers between devices, exchange(): lax.all_to_all(blocks, 'pair', split_axis=0, concat_axis=0, tiled=True)  12.8 us
    all_to_all x2, starting transfers between devices, exchange(): lax.all_to_all(blocks, 'pair', split_axis=0, concat_axis=0, tiled=True)  12.5 us
    pallas_call x1, Pallas kernels, pack(): pl.pallas_call(functools.partial(pack_kernel, dims), grid=(steps,), in_sp...  9.79 us
    pallas_call x1, Pallas kernels, left_half(): pl.pallas_call(functools.partial(left_kernel, dims), in_specs=[VMEM], out...  8.9 us
    unnamed x16, local copies, waits for them, and re-layouts  6.06 us
    ppermute x1, waiting for transfers between devices, body(): lax.ppermute(give, 'chol', CORE_SWAP)  4.28 us
  transfers between devices with their start and end apart: 7, of which 5 were waited for; matrix products, arithmetic and copies ran while one was open for 3% of the time, Pallas kernels for 15%

profile of v2, /device:TPU:1, one launch (start us, length us, event | category | flops | bytes accessed | tf_op | source)
XLA Modules:
  0.0 171.6 jit_solution(13917206072044938750)
XLA Ops:
  0.0 1.0 fusion.7
  1.0 0.1 maximum_select_fusion.1
  1.1 0.1 reshape.60
  1.2 9.8 %shard_map.46 = (bf16[512,4096]{1,0:T(8,128)(2,1)}, bf16[256,4096]{1,0:T(8,128)(2,1)S(1)}) custom-call(bf16[4000,640]{1,0:T(8,128)(2,1)} %bitcast.23, bf16[8,4096]{1,0:T(8,128)(2,1)S(1)} %pad.4.left_ref), custom_call_target="tpu_custom_call" | custom-call | tf_op jit(solution)/shard_map/pallas_call | solution.py:100
  11.0 0.0 copy-start.1
  11.0 59.5 %all_to_all.15 = bf16[32,16,4096]{2,1,0:T(8,128)(2,1)} all-to-all(bf16[32,16,4096]{2,1,0:T(8,128)(2,1)} %bitcast.24), channel_id=1, replica_groups=mesh['pair'=32,'chol'=4] {'pair'}, dimensions={0} | all-to-all | bytes 8388608 | tf_op jit(solution)/shard_map/all_to_all | solution.py:21
  70.6 0.0 copy-done.1
  70.6 2.0 %shard_map.47 = bf16[256,4096]{1,0:T(8,128)(2,1)} custom-call(bf16[512,4096]{1,0:T(8,128)(2,1)} %bitcast.17, bf16[256,4096]{1,0:T(8,128)(2,1)} %copy-done.1), custom_call_target="tpu_custom_call", output_to_operand_aliasing={{}: (1, {})} | custom-call | tf_op jit(solution)/shard_map/pallas_call | solution.py:139
  72.5 4.6 %all-to-all-start.1 = ((bf16[32,8,4096]{2,1,0:T(8,128)(2,1)}), bf16[32,8,4096]{2,1,0:T(8,128)(2,1)S(1)}, u32[]{:S(2)}, u32[]{:S(2)}) async-start(bf16[32,8,4096]{2,1,0:T(8,128)(2,1)} %bitcast.20), calls=%async_computation.1 | async-start | bytes 4194304 | tf_op jit(solution)/shard_map/all_to_all | solution.py:21
  77.1 0.0 copy-start
  77.2 2.2 %copy-done = bf16[32,16,4096]{2,1,0:T(8,128)(2,1)S(1)} copy-done((bf16[32,16,4096]{2,1,0:T(8,128)(2,1)S(1)}, bf16[32,16,4096]{2,1,0:T(8,128)(2,1)}, u32[]{:S(2)}) %copy-start) | copy-done | bytes 4194328
  79.3 8.9 %shard_map.48.mine_ref = bf16[800,640]{1,0:T(8,128)(2,1)S(1)} custom-call(bf16[512,4096]{1,0:T(8,128)(2,1)S(1)} %bitcast.19), custom_call_target="tpu_custom_call" | custom-call | tf_op jit(solution)/shard_map/pallas_call | solution.py:167
  88.2 2.8 %collective-permute-start = (bf16[800,640]{1,0:T(8,128)(2,1)S(1)}, bf16[800,640]{1,0:T(8,128)(2,1)S(1)}, u32[]{:S(2)}, u32[]{:S(2)}) collective-permute-start(bf16[800,640]{1,0:T(8,128)(2,1)S(1)} %shard_map.48.mine_ref), channel_id=1, source_target_pairs={{0,1},{1,0},{2,3},{3,2},{4,5},{5,4},{6,7},{7,6},{8,9},{9,8},{10,11... | collective-permute-start | bytes 3072008 | tf_op jit(solution)/shard_map/ppermute | solution.py:338
  91.0 2.3 %collective-permute-done.other_ref = bf16[800,640]{1,0:T(8,128)(2,1)S(1)} collective-permute-done((bf16[800,640]{1,0:T(8,128)(2,1)S(1)}, bf16[800,640]{1,0:T(8,128)(2,1)S(1)}, u32[]{:S(2)}, u32[]{:S(2)}) %collective-permute-start) | collective-permute-done | bytes 1024032 | tf_op jit(solution)/shard_map/ppermute | solution.py:338
  93.3 17.5 %shard_map.49.refs_0_ = f32[1280,896]{1,0:T(8,128)} custom-call(bf16[512,4096]{1,0:T(8,128)(2,1)} %bitcast.18, bf16[800,640]{1,0:T(8,128)(2,1)S(1)} %shard_map.48.mine_ref, bf16[800,640]{1,0:T(8,128)(2,1)S(1)} %collective-permute-done.other_ref), custom_call_target="tpu_custom_call" | custom-call | flops 7864320000 | bytes 11264000 | tf_op jit(solution)/shard_map/pallas_call | solution.py:263
  110.8 0.0 copy-start.3
  110.8 1.0 copy-done.3
  111.8 0.0 all-to-all-done.1
  111.8 0.0 copy-start.4
  111.8 1.2 copy-done.4
  113.0 13.1 %shard_map.50 = (f32[640,896]{1,0:T(8,128)}, f32[640,896]{1,0:T(8,128)}) custom-call(bf16[256,4096]{1,0:T(8,128)(2,1)S(1)} %bitcast.21, bf16[800,640]{1,0:T(8,128)(2,1)S(1)} %shard_map.48.mine_ref, bf16[800,640]{1,0:T(8,128)(2,1)S(1)} %copy-done.4, f32[1280,896]{1,0:T(8,128)} %shard_map.49.refs_0_), custom_call_target="tpu_custom_call" | custom-call | flops 5242880000 | bytes 10240000 | tf_op jit(solution)/shard_map/pallas_call | solution.py:263
  126.1 0.4 collective-permute-start.1
  126.5 4.3 %collective-permute-done.1.other_ref = f32[640,896]{1,0:T(8,128)S(1)} collective-permute-done((f32[640,896]{1,0:T(8,128)}, f32[640,896]{1,0:T(8,128)S(1)}, u32[]{:S(2)}, u32[]{:S(2)}) %collective-permute-start.1) | collective-permute-done | bytes 2293792 | tf_op jit(solution)/shard_map/ppermute | solution.py:345
  130.8 0.0 copy-start.2
  130.8 1.6 copy-done.2
  132.4 3.3 %shard_map.51 = bf16[32,5,4,800]{3,2,1,0:T(4,128)(2,1)} custom-call(f32[640,896]{1,0:T(8,128)S(1)} %copy-done.2, f32[640,896]{1,0:T(8,128)S(1)} %collective-permute-done.1.other_ref), custom_call_target="tpu_custom_call" | custom-call | tf_op jit(solution)/shard_map/pallas_call | solution.py:301
  135.7 7.8 %all-to-all-start.2 = ((bf16[32,5,4,800]{3,2,1,0:T(4,128)(2,1)}), bf16[32,5,4,800]{3,2,1,0:T(4,128)(2,1)S(1)}, u32[]{:S(2)}, u32[]{:S(2)}) async-start(bf16[32,5,4,800]{3,2,1,0:T(4,128)(2,1)} %shard_map.51), calls=%async_computation.2 | async-start | bytes 2293760 | tf_op jit(solution)/shard_map/all_to_all | solution.py:21
  143.5 0.1 slice_bitcast_fusion
  143.7 0.1 slice.29
  143.7 0.1 reshape.67
  143.9 0.1 reshape.66
  144.0 0.0 copy-start.6
  144.0 0.0 copy-start.7
  144.0 0.0 copy-start.5
  144.0 4.0 %fusion.3 = f32[8,5,800]{2,0,1:T(8,128)S(1)} fusion(bf16[5,800,640]{2,1,0:T(8,128)(2,1)} %param.5, bf16[8,256]{1,0:T(8,128)(2,1)S(1)} %reshape.67, bf16[8,384]{1,0:T(8,128)(2,1)S(1)} %reshape.66), kind=kOutput, calls=%fused_computation.11 | convolution fusion | flops 40980480 | bytes 5258240 | tf_op jit(solution)/shard_map/iap,rp->ria/dot_general | solution.py:358
  148.1 0.7 collective-permute-start.2
  148.8 12.8 %all-to-all-done.2 = bf16[32,5,4,800]{3,2,1,0:T(4,128)(2,1)S(1)} async-done(((bf16[32,5,4,800]{3,2,1,0:T(4,128)(2,1)}), bf16[32,5,4,800]{3,2,1,0:T(4,128)(2,1)S(1)}, u32[]{:S(2)}, u32[]{:S(2)}) %all-to-all-start.2) | async-done | bytes 1024032 | tf_op jit(solution)/shard_map/all_to_all | solution.py:21
  161.6 0.5 convert_reduce_fusion
  162.1 0.0 collective-permute-done.2
  162.1 2.5 %collective-permute-start.3 = (f32[4,5,800]{2,0,1:T(4,128)S(1)}, f32[4,5,800]{2,0,1:T(4,128)S(1)}, u32[]{:S(2)}, u32[]{:S(2)}) collective-permute-start(f32[4,5,800]{2,0,1:T(4,128)S(1)} %fusion.2), channel_id=1, source_target_pairs={{0,2},{2,0},{1,3},{3,1},{4,6},{6,4},{5,7},{7,5},{8,10},{10,8},{9,1... | collective-permute-start | bytes 192008 | tf_op jit(solution)/shard_map/ppermute | solution.py:362
  164.6 2.2 %collective-permute-done.3 = f32[4,5,800]{2,0,1:T(4,128)S(1)} collective-permute-done((f32[4,5,800]{2,0,1:T(4,128)S(1)}, f32[4,5,800]{2,0,1:T(4,128)S(1)}, u32[]{:S(2)}, u32[]{:S(2)}) %collective-permute-start.3) | collective-permute-done | bytes 64032 | tf_op jit(solution)/shard_map/ppermute | solution.py:362
  166.9 3.0 %collective-permute-start.4 = (f32[4,5,800]{2,0,1:T(4,128)S(1)}, f32[4,5,800]{2,0,1:T(4,128)S(1)}, u32[]{:S(2)}, u32[]{:S(2)}) collective-permute-start(f32[4,5,800]{2,0,1:T(4,128)S(1)} %add.12), channel_id=1, source_target_pairs={{0,1},{1,0},{2,3},{3,2},{4,5},{5,4},{6,7},{7,6},{8,9},{9,8},{10,11... | collective-permute-start | bytes 192008 | tf_op jit(solution)/shard_map/ppermute | solution.py:363
  169.9 0.0 copy-done.6
  169.9 0.0 copy-done.7
  169.9 0.1 broadcast_subtract_fusion
  170.0 0.8 collective-permute-done.4
  170.8 0.0 copy-done.5
  170.9 0.7 fusion
  (6 shorter events, 0.1 us)
Async XLA Ops:
  11.0 59.5 %copy-start.1 = (bf16[256,4096]{1,0:T(8,128)(2,1)}, bf16[256,4096]{1,0:T(8,128)(2,1)S(1)}, u32[]{:S(2)}) copy-start(bf16[256,4096]{1,0:T(8,128)(2,1)S(1)} %get-tuple-element.12.send_ref) | copy-start | bytes 6291460
  72.5 39.3 %all-to-all-start.1 = ((bf16[32,8,4096]{2,1,0:T(8,128)(2,1)}), bf16[32,8,4096]{2,1,0:T(8,128)(2,1)S(1)}, u32[]{:S(2)}, u32[]{:S(2)}) async-start(bf16[32,8,4096]{2,1,0:T(8,128)(2,1)} %bitcast.20), calls=%async_computation.1 | async-start | bytes 4194304 | tf_op jit(solution)/shard_map/all_to_all | solution.py:21
  77.1 2.2 %copy-start = (bf16[32,16,4096]{2,1,0:T(8,128)(2,1)S(1)}, bf16[32,16,4096]{2,1,0:T(8,128)(2,1)}, u32[]{:S(2)}) copy-start(bf16[32,16,4096]{2,1,0:T(8,128)(2,1)} %all_to_all.15) | copy-start | bytes 12582916
  88.2 5.0 %collective-permute-start = (bf16[800,640]{1,0:T(8,128)(2,1)S(1)}, bf16[800,640]{1,0:T(8,128)(2,1)S(1)}, u32[]{:S(2)}, u32[]{:S(2)}) collective-permute-start(bf16[800,640]{1,0:T(8,128)(2,1)S(1)} %shard_map.48.mine_ref), channel_id=1, source_target_pairs={{0,1},{1,0},{2,3},{3,2},{4,5},{5,4},{6,7},{7,6},{8,9},{9,8},{10,11... | collective-permute-start | bytes 3072008 | tf_op jit(solution)/shard_map/ppermute | solution.py:338
  110.8 1.0 copy-start.3
  111.8 1.2 copy-start.4
  126.1 4.7 %collective-permute-start.1 = (f32[640,896]{1,0:T(8,128)}, f32[640,896]{1,0:T(8,128)S(1)}, u32[]{:S(2)}, u32[]{:S(2)}) collective-permute-start(f32[640,896]{1,0:T(8,128)} %get-tuple-element.14), channel_id=1, source_target_pairs={{0,1},{1,0},{2,3},{3,2},{4,5},{5,4},{6,7},{7,6},{8,9},{9,8},{10,11... | collective-permute-start | bytes 6881288 | tf_op jit(solution)/shard_map/ppermute | solution.py:345
  130.8 1.6 copy-start.2
  135.7 25.9 %all-to-all-start.2 = ((bf16[32,5,4,800]{3,2,1,0:T(4,128)(2,1)}), bf16[32,5,4,800]{3,2,1,0:T(4,128)(2,1)S(1)}, u32[]{:S(2)}, u32[]{:S(2)}) async-start(bf16[32,5,4,800]{3,2,1,0:T(4,128)(2,1)} %shard_map.51), calls=%async_computation.2 | async-start | bytes 2293760 | tf_op jit(solution)/shard_map/all_to_all | solution.py:21
  144.0 25.9 %copy-start.6 = (f32[800]{0:T(1024)S(1)}, f32[800]{0:T(1024)}, u32[]{:S(2)}) copy-start(f32[800]{0:T(1024)} %param.7) | copy-start | bytes 9604
  144.0 25.9 %copy-start.7 = (f32[5]{0:T(128)S(1)}, f32[5]{0:T(128)}, u32[]{:S(2)}) copy-start(f32[5]{0:T(128)} %param.6) | copy-start | bytes 64
  144.0 26.8 %copy-start.5 = (bf16[8,5,800]{2,0,1:T(8,128)(2,1)S(1)}, bf16[8,5,800]{2,0,1:T(8,128)(2,1)}, u32[]{:S(2)}) copy-start(bf16[8,5,800]{2,0,1:T(8,128)(2,1)} %param.4) | copy-start | bytes 192004
  148.1 14.0 %collective-permute-start.2 = (f32[4,5,800]{2,0,1:T(4,128)S(1)}, f32[4,5,800]{2,0,1:T(4,128)S(1)}, u32[]{:S(2)}, u32[]{:S(2)}) collective-permute-start(f32[4,5,800]{2,0,1:T(4,128)S(1)} %slice.31), channel_id=1, source_target_pairs={{0,1},{1,0},{2,3},{3,2},{4,5},{5,4},{6,7},{7,6},{8,9},{9,8},{10,11... | collective-permute-start | bytes 192008 | tf_op jit(solution)/shard_map/ppermute | solution.py:359
  162.1 4.8 %collective-permute-start.3 = (f32[4,5,800]{2,0,1:T(4,128)S(1)}, f32[4,5,800]{2,0,1:T(4,128)S(1)}, u32[]{:S(2)}, u32[]{:S(2)}) collective-permute-start(f32[4,5,800]{2,0,1:T(4,128)S(1)} %fusion.2), channel_id=1, source_target_pairs={{0,2},{2,0},{1,3},{3,1},{4,6},{6,4},{5,7},{7,5},{8,10},{10,8},{9,1... | collective-permute-start | bytes 192008 | tf_op jit(solution)/shard_map/ppermute | solution.py:362
  166.9 3.9 %collective-permute-start.4 = (f32[4,5,800]{2,0,1:T(4,128)S(1)}, f32[4,5,800]{2,0,1:T(4,128)S(1)}, u32[]{:S(2)}, u32[]{:S(2)}) collective-permute-start(f32[4,5,800]{2,0,1:T(4,128)S(1)} %add.12), channel_id=1, source_target_pairs={{0,1},{1,0},{2,3},{3,2},{4,5},{5,4},{6,7},{7,6},{8,9},{9,8},{10,11... | collective-permute-start | bytes 192008 | tf_op jit(solution)/shard_map/ppermute | solution.py:363

commit v3 on v2

v3 whole, which is shorter than its diff:
```python
import functools

import jax
import jax.numpy as jnp
from jax import lax
from jax.experimental import pallas as pl
from jax.experimental.pallas import tpu as pltpu
from jax.sharding import PartitionSpec as P


CORE_SWAP = [(0, 1), (1, 0), (2, 3), (3, 2)]
FAR_SWAP = [(0, 2), (2, 0), (1, 3), (3, 1)]
LANES = 128
FIRST = 12
CHUNK = 1024
VMEM = pl.BlockSpec(memory_space=pltpu.VMEM)
HBM = pl.BlockSpec(memory_space=pl.ANY)
MIB = 1024 * 1024
HIGH = 48 * MIB
VLIM1 = 60 * MIB
VLIM2 = 40 * MIB
VLIM3 = 16 * MIB
NT = (((1,), (1,)), ((), ()))


def exchange(blocks):
    return lax.all_to_all(blocks, "pair", split_axis=0, concat_axis=0, tiled=True)


def up(value, unit):
    return pl.cdiv(value, unit) * unit


def iota(shape, axis):
    return lax.broadcasted_iota(jnp.int32, shape, axis)


def one_hot(flag):
    return jnp.where(flag, 1.0, 0.0).astype(jnp.bfloat16)


def dot(a, b):
    return jnp.dot(a, b, preferred_element_type=jnp.float32)


def pack_kernel(
    dims, core_ref, factors_ref, left_ref, first_ref, second_ref, sums, pick, lay, keep
):
    ranks, share, rows, roots = dims
    half = roots // 2
    rest = share - FIRST
    pitch = FIRST + half
    cut = ranks * FIRST
    aux = ranks * share
    k = pl.program_id(0)
    last = pl.cdiv(rows, CHUNK) - 1

    def some(size):
        block = factors_ref[:size, :]
        left = left_ref[:, :size]
        moved = lax.dot_general(pick[...], block[:, :cut], NT, preferred_element_type=jnp.float32)
        first_ref[:, :size] = (moved + dot(lay[...], left)).astype(jnp.bfloat16)
        moved = lax.dot_general(keep[...], block[:, cut:], NT, preferred_element_type=jnp.float32)
        second_ref[:, :size] = moved.astype(jnp.bfloat16)
        return dot(left, block)

    @pl.when(k == 0)
    def _():
        row, col = iota((ranks * pitch, cut), 0), iota((ranks * pitch, cut), 1)
        pick[...] = one_hot((row % pitch < FIRST) & (col == row // pitch * FIRST + row % pitch))
        row, col = iota((ranks * pitch, roots), 0), iota((ranks * pitch, roots), 1)
        at = row % pitch - FIRST
        lay[...] = one_hot((at >= 0) & (at + core_ref[0] * half == col))
        keep[...] = one_hot(iota((aux - cut, aux - cut), 0) == iota((aux - cut, aux - cut), 1))
        sums[...] = some(CHUNK)

    @pl.when((k > 0) & (k < last))
    def _():
        sums[...] += some(CHUNK)

    @pl.when(k == last)
    def _():
        size = rows - last * CHUNK
        left_over = sums[...] + some(size)
        row, col = iota((ranks * pitch, roots), 0), iota((ranks * pitch, roots), 1)
        lay_root = one_hot(row % pitch == col)
        row, col = iota((ranks * pitch, aux), 0), iota((ranks * pitch, aux), 1)
        owner = jnp.where(col < cut, col // FIRST, (col - cut) // rest)
        mine = owner == row // pitch
        spare = CHUNK - size
        row, col = iota((aux, spare), 0), iota((aux, spare), 1)
        slot = jnp.where(row < cut, row % FIRST, FIRST + (row - cut) % rest)
        extra = jnp.zeros((ranks * pitch, spare), jnp.float32)
        for t in range(3):
            term = left_over.astype(jnp.bfloat16)
            left_over = left_over - term.astype(jnp.float32)
            spread = jnp.where(mine, dot(lay_root, term), 0.0).astype(jnp.bfloat16)
            extra = extra + dot(spread, one_hot(col == t * share + slot))
        first_ref[:, size:] = extra.astype(jnp.bfloat16)
        second_ref[:, size:] = jnp.zeros((ranks * rest, spare), jnp.bfloat16)


def pack(factors, lefts, core, dims):
    ranks, share, rows, roots = dims
    pitch = FIRST + roots // 2
    rest = share - FIRST
    steps = pl.cdiv(rows, CHUNK)
    return pl.pallas_call(
        functools.partial(pack_kernel, dims),
        grid=(steps,),
        in_specs=[
            pl.BlockSpec(memory_space=pltpu.SMEM),
            pl.BlockSpec((CHUNK, ranks * share), lambda k: (k, 0)),
            pl.BlockSpec((roots, CHUNK), lambda k: (0, k)),
        ],
        out_specs=[
            pl.BlockSpec((ranks * pitch, CHUNK), lambda k: (0, k)),
            pl.BlockSpec((ranks * rest, CHUNK), lambda k: (0, k)),
        ],
        out_shape=[
            jax.ShapeDtypeStruct((ranks * pitch, steps * CHUNK), jnp.bfloat16),
            jax.ShapeDtypeStruct((ranks * rest, steps * CHUNK), jnp.bfloat16),
        ],
        scratch_shapes=[
            pltpu.VMEM((roots, ranks * share), jnp.float32),
            pltpu.VMEM((ranks * pitch, ranks * FIRST), jnp.bfloat16),
            pltpu.VMEM((ranks * pitch, roots), jnp.bfloat16),
            pltpu.VMEM((ranks * rest, ranks * rest), jnp.bfloat16),
        ],
        compiler_params=pltpu.CompilerParams(vmem_limit_bytes=HIGH),
    )(core, factors, lefts)


def coul_kernel(dims, got_ref, send_ref, out_ref):
    ranks, share, rows, roots = dims
    pitch = FIRST + roots // 2
    rest = share - FIRST
    start = rows % LANES
    row, col = iota((roots, ranks * pitch), 0), iota((roots, ranks * pitch), 1)
    sums = dot(one_hot(col % pitch == row), got_ref[...])
    turn = LANES - share
    once = pltpu.roll(sums, turn, 1)
    sums = sums + once + pltpu.roll(once, turn, 1)
    row, col = iota((ranks * rest, roots), 0), iota((ranks * rest, roots), 1)
    laid = dot(one_hot(row % rest == col), sums.astype(jnp.bfloat16)).astype(jnp.bfloat16)
    lane = iota((ranks * rest, LANES), 1)
    out_ref[...] = jnp.where(lane < start, send_ref[...], laid)


def coul_round(got, send, dims):
    _, _, rows, _ = dims
    at = rows // LANES
    return pl.pallas_call(
        functools.partial(coul_kernel, dims),
        grid=(1,),
        in_specs=[
            pl.BlockSpec((got.shape[0], LANES), lambda k: (0, at)),
            pl.BlockSpec((send.shape[0], LANES), lambda k: (0, at)),
        ],
        out_specs=pl.BlockSpec((send.shape[0], LANES), lambda k: (0, at)),
        out_shape=jax.ShapeDtypeStruct(send.shape, send.dtype),
        input_output_aliases={1: 0},
    )(got, send)


def left_kernel(dims, got_ref, out_ref, rows):
    ranks, occ_local, vir, half = dims
    pitch = FIRST + half
    main = ranks * (occ_local - 1)
    row, col = iota((half * ranks, ranks * pitch), 0), iota((half * ranks, ranks * pitch), 1)
    turn = one_hot(col == (row % ranks) * pitch + FIRST + row // ranks)
    for i in range(occ_local):
        part = dot(turn, got_ref[:, i * vir : (i + 1) * vir]).astype(jnp.bfloat16)
        for r in range(half):
            to = r * main + i * ranks if i < occ_local - 1 else half * main + r * ranks
            rows[to : to + ranks, :] = part[r * ranks : (r + 1) * ranks]
    for at in range(0, rows.shape[0], LANES):
        out_ref[:, at : at + LANES] = rows[at : at + LANES, :].T


def left_half(got, dims):
    ranks, occ_local, vir, half = dims
    count = half * ranks * occ_local
    return pl.pallas_call(
        functools.partial(left_kernel, dims),
        in_specs=[VMEM],
        out_specs=VMEM,
        out_shape=jax.ShapeDtypeStruct((vir, count), jnp.bfloat16),
        scratch_shapes=[pltpu.VMEM((count, vir), jnp.bfloat16)],
        compiler_params=pltpu.CompilerParams(vmem_limit_bytes=24 * 1024 * 1024),
    )(got)


def to_tiles(value, out_ref):
    vir = value.shape[1]
    for t in range(out_ref.shape[0]):
        size = min(LANES, vir - t * LANES)
        out_ref[t, :, :size] = value[:, t * LANES : t * LANES + size]


def fetch_old(total_ref, old, sems):
    rows = old.shape[0]
    return pltpu.make_async_copy(total_ref.at[rows : 2 * rows, :], old, sems.at[4])


def slab_kernel(dims, final, recv_ref, mine_ref, other_ref, *refs):
    ranks, share, pitch, occ_local, vir, roots = dims
    if final:
        total_ref, give_ref, zed_ref, rows_e, left, sems, rows_z, zed, old = refs
    else:
        out_ref, left, sems, rows_z, rows_e, zed = refs
    occ = ranks * occ_local
    main = occ - ranks
    packed = main // ranks
    half = roots // 2

    @pl.when(pl.program_id(0) == 0)
    def _():
        copies = []
        for h, ref in enumerate((mine_ref, other_ref)):
            for at, size, to in (
                (0, half * main, h * half * main),
                (half * main, half * ranks, roots * main + h * half * ranks),
            ):
                copies.append(
                    pltpu.make_async_copy(
                        ref.at[:, at : at + size],
                        left.at[:, to : to + size],
                        sems.at[len(copies)],
                    )
                )
        for copy in copies:
            copy.start()
        if final:
            fetch_old(total_ref, old, sems).start()

        group = min(ranks, 256 // pitch)
        piece = group * pitch
        row, col = iota((group * share, piece), 0), iota((group * share, piece), 1)
        turn = one_hot(col == (row % group) * pitch + row // group)
        for at in range(ranks // group):
            for i in range(occ_local):
                part = recv_ref[at * piece : (at + 1) * piece, i * vir : (i + 1) * vir]
                part = dot(turn, part).astype(jnp.bfloat16)
                for s in range(share):
                    rows = part[s * group : (s + 1) * group]
                    to = s * occ + i * ranks + at * group
                    rows_z[to : to + group, :] = rows
                    if i < occ_local - 1:
                        to = s * main + i * ranks + at * group
                    else:
                        to = share * main + s * ranks + at * group
                    rows_e[to : to + group, :] = rows

        for copy in copies:
            copy.wait()
        place = iota((occ, main), 1) // ranks

        def put(r, to, value):
            if final and r < half:
                zed_ref[r * occ : (r + 1) * occ, pl.ds(to, main)] = value
            else:
                at = r - half if final else r
                zed[at * occ : (at + 1) * occ, pl.ds(to, main)] = value

        def some_vectors(k, carry):
            at = pl.multiple_of(k * packed * occ, packed * occ)
            z = dot(rows_z[pl.ds(at, packed * occ), :], left[...]).astype(jnp.bfloat16)
            for r in range(roots):
                low = roots * main + (r // packed) * main
                rest = jnp.zeros((occ, main), jnp.bfloat16)
                for s in range(packed):
                    zs = z[s * occ : (s + 1) * occ]
                    to = pl.multiple_of(k * packed * main, packed * main) + s * main
                    put(r, to, zs[:, r * main : (r + 1) * main])
                    turned = zs[:, low : low + main]
                    shift = (s - r % packed) % packed * ranks
                    if shift:
                        turned = pltpu.roll(turned, shift, 1)
                    rest = jnp.where(place == s, turned, rest)
                put(r, pl.multiple_of(share * main + k * main, main), rest)
            return carry

        lax.fori_loop(0, share // packed, some_vectors, 0)

    if final:
        part = dot(zed[...], rows_e[...])
        fetch_old(total_ref, old, sems).wait()
        to_tiles(old[:, :vir] + part, give_ref)
    else:
        step = out_ref.shape[0]
        at = pl.multiple_of(pl.program_id(0) * step, step)
        out_ref[:, :vir] = dot(zed[pl.ds(at, step), :], rows_e[...])


def slab_product(recv, mine, other, total, dims):
    ranks, share, _, occ_local, vir, roots = dims
    occ = ranks * occ_local
    width = up(vir, LANES)
    final = total is not None
    steps = 1 if final else 4
    rows = roots * occ // (2 if final else 4)
    args = [recv, mine, other] + ([total] if final else [])
    return pl.pallas_call(
        functools.partial(slab_kernel, dims, final),
        grid=(steps,),
        in_specs=[VMEM, HBM, HBM] + ([HBM] if final else []),
        out_specs=[VMEM, VMEM, VMEM] if final else pl.BlockSpec((rows, width), lambda k: (k, 0)),
        out_shape=[
            jax.ShapeDtypeStruct((width // LANES, rows, LANES), jnp.float32),
            jax.ShapeDtypeStruct((rows, share * occ), jnp.bfloat16),
            jax.ShapeDtypeStruct((share * occ, vir), jnp.bfloat16),
        ]
        if final
        else jax.ShapeDtypeStruct((roots * occ, width), jnp.float32),
        scratch_shapes=[
            pltpu.VMEM((vir, roots * occ), jnp.bfloat16),
            pltpu.SemaphoreType.DMA((5,)),
            pltpu.VMEM((share * occ, vir), jnp.bfloat16),
        ]
        + ([] if final else [pltpu.VMEM((share * occ, vir), jnp.bfloat16)])
        + [pltpu.VMEM((rows if final else roots * occ, share * occ), jnp.bfloat16)]
        + ([pltpu.VMEM((rows, width), jnp.float32)] if final else []),
        compiler_params=pltpu.CompilerParams(vmem_limit_bytes=VLIM2 if final else VLIM1),
        cost_estimate=pl.CostEstimate(
            flops=4 * share * occ * roots * occ * vir,
            transcendentals=0,
            bytes_accessed=2 * share * occ * vir + 8 * roots * occ * vir,
        ),
    )(*args)


def keep_kernel(zed_ref, rows_ref, total_ref, out_ref):
    vir = rows_ref.shape[1]
    to_tiles(total_ref[:, :vir] + dot(zed_ref[...], rows_ref[...]), out_ref)


def keep_product(zed, rows_e, total):
    rows, width = zed.shape[0], total.shape[1]
    step = rows // 2
    return pl.pallas_call(
        keep_kernel,
        grid=(2,),
        in_specs=[
            pl.BlockSpec((step, zed.shape[1]), lambda k: (k, 0)),
            VMEM,
            pl.BlockSpec((step, width), lambda k: (k, 0)),
        ],
        out_specs=pl.BlockSpec((width // LANES, step, LANES), lambda k: (0, k, 0)),
        out_shape=jax.ShapeDtypeStruct((width // LANES, rows, LANES), jnp.float32),
        compiler_params=pltpu.CompilerParams(vmem_limit_bytes=VLIM3),
        cost_estimate=pl.CostEstimate(
            flops=2 * rows * zed.shape[1] * width,
            transcendentals=0,
            bytes_accessed=8 * rows * width + 4 * rows * zed.shape[1],
        ),
    )(zed, rows_e, total)


def merge_kernel(keep_ref, other_ref, out_ref, tiles):
    ranks, occ_local, half, vir = out_ref.shape
    occ = ranks * occ_local
    for t in range(tiles.shape[0]):
        tiles[t] = keep_ref[t] + other_ref[t]
    for d in range(ranks):
        for i in range(occ_local):
            for t in range(keep_ref.shape[0]):
                at = t * LANES
                size = min(LANES, vir - at)
                rows = tiles[t, pl.ds(i * ranks + d, half, stride=occ), :]
                out_ref[d, i, :, at : at + size] = rows[:, :size].astype(jnp.bfloat16)


def merge(keep, other, shape):
    return pl.pallas_call(
        merge_kernel,
        in_specs=[VMEM, VMEM],
        out_specs=VMEM,
        out_shape=jax.ShapeDtypeStruct(shape, jnp.bfloat16),
        scratch_shapes=[pltpu.VMEM(keep.shape, jnp.float32)],
        compiler_params=pltpu.CompilerParams(vmem_limit_bytes=24 * MIB),
    )(keep, other)


def body(left_vectors, chol_factors, eps_occ, eps_vir):
    roots, occ_local, vir = left_vectors.shape
    aux_local = chol_factors.shape[2]
    ranks = lax.axis_size("pair")
    share = aux_local // ranks
    rest = share - FIRST
    rows = occ_local * vir
    half = roots // 2
    core = lax.rem(lax.axis_index("chol"), 2)
    dims = (ranks, share, rows, roots)

    lefts = jnp.pad(left_vectors.reshape(roots, rows), ((0, 0), (0, up(rows, CHUNK) - rows)))
    first_send, second_send = pack(
        chol_factors.reshape(rows, aux_local), lefts, core.reshape(1), dims
    )

    pitch = FIRST + half
    first = exchange(first_send.reshape(ranks, pitch, -1)).reshape(ranks * pitch, -1)
    second_send = coul_round(first, second_send, dims)
    second = exchange(second_send.reshape(ranks, rest, -1)).reshape(ranks * rest, -1)
    mine = left_half(first, (ranks, occ_local, vir, half))
    other = lax.ppermute(mine, "chol", CORE_SWAP)

    total = slab_product(
        first, mine, other, None, (ranks, FIRST, pitch, occ_local, vir, roots)
    )
    give, zed, rows_e = slab_product(
        second, mine, other, total, (ranks, rest, rest, occ_local, vir, roots)
    )
    got = lax.ppermute(give, "chol", CORE_SWAP)
    keep = keep_product(zed, rows_e, total)

    merged = merge(keep, got, (ranks, occ_local, half, vir))
    merged, second = lax.optimization_barrier((merged, second))
    pieces = exchange(merged)
    exch = jnp.sum(pieces.astype(jnp.float32), axis=0).transpose(1, 0, 2)

    coul_vec = second[:, rows : rows + share].reshape(ranks, roots, share).transpose(1, 0, 2)
    coul_vec = jnp.concatenate(
        [
            coul_vec[:, :, :FIRST].reshape(roots, ranks * FIRST),
            coul_vec[:, :, FIRST:].reshape(roots, ranks * rest),
        ],
        axis=1,
    )
    coulomb = jnp.einsum("iap,rp->ria", chol_factors, coul_vec, preferred_element_type=jnp.float32)
    coul_keep = lax.dynamic_slice_in_dim(coulomb, core * half, half, 0)
    coul_give = lax.dynamic_slice_in_dim(coulomb, (1 - core) * half, half, 0)
    coul_keep = coul_keep + lax.ppermute(coul_give, "chol", CORE_SWAP)

    part = 2.0 * coul_keep - exch
    part = part + lax.ppermute(part, "chol", FAR_SWAP)
    rest_part = lax.ppermute(part, "chol", CORE_SWAP)
    summed = jnp.where(
        core == 0,
        jnp.concatenate([part, rest_part], axis=0),
        jnp.concatenate([rest_part, part], axis=0),
    )
    diagonal_part = (eps_vir[None, None, :] - eps_occ[None, :, None]) * left_vectors.astype(
        jnp.float32
    )
    return diagonal_part + summed


def solution(mesh):
    placed = (P(None, "pair", None), P("pair", None, "chol"), P("pair"), P())
    return jax.shard_map(
        body, mesh=mesh, in_specs=placed, out_specs=P(None, "pair", None), check_vma=False
    )
```

time: 172 us -> 157 us (0.913)
  Pallas kernels: 54.6 us -> 44.6 us
  local copies, waits for them, and re-layouts: 7.68 us -> 5.09 us
    pallas_call x1, Pallas kernels: 8.9 us -> 1.37 us  [left_half(): pl.pallas_call(functools.partial(left_kernel, dims), in_specs=[VMEM], out...]
    pallas_call x2, Pallas kernels: 30.6 us -> 26.5 us  [slab_product(): pl.pallas_call(functools.partial(slab_kernel, dims, final), grid=(steps,)...]
    all_to_all x2, starting transfers between devices: 12.5 us -> 8.41 us  [exchange(): lax.all_to_all(blocks, 'pair', split_axis=0, concat_axis=0, tiled=True)]
    ppermute x2, starting transfers between devices: 1.11 us -> 3.9 us  [the longest x1 3.16 us: body(): got = lax.ppermute(give, 'chol', CORE_SWAP)]
    ppermute x2, waiting for transfers between devices: 4.28 us -> 1.87 us  [the longest x1 1.87 us: body(): got = lax.ppermute(give, 'chol', CORE_SWAP)]
    pallas_call x0 -> x1, Pallas kernels: none -> 2.19 us  [keep_product(): pl.pallas_call(keep_kernel, grid=(2,), in_specs=[pl.BlockSpec((step, zed....]
    unnamed x16 -> x19, local copies, waits for them, and re-layouts: 6.06 us -> 4.48 us
  transfers between devices with their start and end apart: 7 -> 7, of which waited for: 5 -> 6; matrix products, arithmetic and copies ran while one was open for 3% -> 3% of each run, Pallas kernels for 15% -> 14%
where the time goes in v3:
time: 157 us
  blocking collectives  60.4 us (38%)
  Pallas kernels  44.6 us (28%)
  waiting for transfers between devices  21 us (13%)
  starting transfers between devices  20.2 us (13%)
  local copies, waits for them, and re-layouts  5.09 us (3%)
  matrix products  3.99 us (3%)
    all_to_all x1, blocking collectives, exchange(): lax.all_to_all(blocks, 'pair', split_axis=0, concat_axis=0, tiled=True)  60.4 us
    pallas_call x2, Pallas kernels, slab_product(): pl.pallas_call(functools.partial(slab_kernel, dims, final), grid=(steps,)...  26.5 us
    all_to_all x2, waiting for transfers between devices, exchange(): lax.all_to_all(blocks, 'pair', split_axis=0, concat_axis=0, tiled=True)  13.7 us
    pallas_call x1, Pallas kernels, pack(): pl.pallas_call(functools.partial(pack_kernel, dims), grid=(steps,), in_sp...  9.25 us
    all_to_all x2, starting transfers between devices, exchange(): lax.all_to_all(blocks, 'pair', split_axis=0, concat_axis=0, tiled=True)  8.41 us
    unnamed x19, local copies, waits for them, and re-layouts  4.48 us
    dot_general x1, matrix products, body(): jnp.einsum('iap,rp->ria', chol_factors, coul_vec, preferred_element_type=...  3.99 us
    pallas_call x1, Pallas kernels, merge(): pl.pallas_call(merge_kernel, in_specs=[VMEM, VMEM], out_specs=VMEM, out_s...  3.28 us
  transfers between devices with their start and end apart: 7, of which 6 were waited for; matrix products, arithmetic and copies ran while one was open for 3% of the time, Pallas kernels for 14%

profile of v3, /device:TPU:1, one launch (start us, length us, event | category | flops | bytes accessed | tf_op | source)
XLA Modules:
  0.0 156.7 jit_solution(15818242828353912800)
XLA Ops:
  0.0 0.9 copy.9
  0.9 0.1 reshape.64
  1.0 9.3 %shard_map.46 = (bf16[512,4096]{1,0:T(8,128)(2,1)}, bf16[256,4096]{1,0:T(8,128)(2,1)S(1)}) custom-call(s32[1]{0:T(128)} %bitcast.core_ref, bf16[4000,640]{1,0:T(8,128)(2,1)} %bitcast.26, bf16[8,4096]{1,0:T(8,128)(2,1)S(1)} %pad.4.left_ref), custom_call_target="tpu_custom_call" | custom-call | tf_op jit(solution)/shard_map/pallas_call | solution.py:108
  10.3 0.0 copy-start.1
  10.3 60.4 %all_to_all.15 = bf16[32,16,4096]{2,1,0:T(8,128)(2,1)} all-to-all(bf16[32,16,4096]{2,1,0:T(8,128)(2,1)} %bitcast.27), channel_id=1, replica_groups=mesh['pair'=32,'chol'=4] {'pair'}, dimensions={0} | all-to-all | bytes 8388608 | tf_op jit(solution)/shard_map/all_to_all | solution.py:27
  70.7 0.0 copy-done.1
  70.7 2.0 %shard_map.47 = bf16[256,4096]{1,0:T(8,128)(2,1)} custom-call(bf16[512,4096]{1,0:T(8,128)(2,1)} %bitcast.18, bf16[256,4096]{1,0:T(8,128)(2,1)} %copy-done.1), custom_call_target="tpu_custom_call", output_to_operand_aliasing={{}: (1, {})} | custom-call | tf_op jit(solution)/shard_map/pallas_call | solution.py:153
  72.7 4.0 %all-to-all-start.1 = ((bf16[32,8,4096]{2,1,0:T(8,128)(2,1)}), bf16[32,8,4096]{2,1,0:T(8,128)(2,1)S(1)}, u32[]{:S(2)}, u32[]{:S(2)}) async-start(bf16[32,8,4096]{2,1,0:T(8,128)(2,1)} %bitcast.21), calls=%async_computation.1 | async-start | bytes 4194304 | tf_op jit(solution)/shard_map/all_to_all | solution.py:27
  76.7 0.0 copy-start
  76.7 2.2 %copy-done = bf16[32,16,4096]{2,1,0:T(8,128)(2,1)S(1)} copy-done((bf16[32,16,4096]{2,1,0:T(8,128)(2,1)S(1)}, bf16[32,16,4096]{2,1,0:T(8,128)(2,1)}, u32[]{:S(2)}) %copy-start) | copy-done | bytes 4194328
  78.9 1.4 shard_map.48.mine_ref
  80.2 0.0 copy-start.2
  80.3 2.3 %collective-permute-start = (bf16[800,640]{1,0:T(8,128)(2,1)S(1)}, bf16[800,640]{1,0:T(8,128)(2,1)}, u32[]{:S(2)}, u32[]{:S(2)}) collective-permute-start(bf16[800,640]{1,0:T(8,128)(2,1)S(1)} %shard_map.48.mine_ref), channel_id=1, source_target_pairs={{0,1},{1,0},{2,3},{3,2},{4,5},{5,4},{6,7},{7,6},{8,9},{9,8},{10,11... | collective-permute-start | bytes 3072008 | tf_op jit(solution)/shard_map/ppermute | solution.py:406
  82.6 2.4 %collective-permute-done.other_ref = bf16[800,640]{1,0:T(8,128)(2,1)} collective-permute-done((bf16[800,640]{1,0:T(8,128)(2,1)S(1)}, bf16[800,640]{1,0:T(8,128)(2,1)}, u32[]{:S(2)}, u32[]{:S(2)}) %collective-permute-start) | collective-permute-done | bytes 1024032 | tf_op jit(solution)/shard_map/ppermute | solution.py:406
  85.0 0.0 copy-done.2
  85.0 18.0 %shard_map.49.refs_0_.total_ref = f32[1280,896]{1,0:T(8,128)} custom-call(bf16[512,4096]{1,0:T(8,128)(2,1)} %bitcast.19, bf16[800,640]{1,0:T(8,128)(2,1)} %copy-done.2, bf16[800,640]{1,0:T(8,128)(2,1)} %collective-permute-done.other_ref), custom_call_target="tpu_custom_call" | custom-call | flops 7864320000 | bytes 11264000 | tf_op jit(solution)/shard_map/pallas_call | solution.py:304
  103.0 0.9 all-to-all-done.1
  103.9 0.0 slice-start
  103.9 1.4 copy-done.3
  105.3 8.5 %shard_map.50 = (f32[7,640,128]{2,1,0:T(8,128)S(1)}, bf16[640,1280]{1,0:T(8,128)(2,1)S(1)}, bf16[1280,800]{1,0:T(8,128)(2,1)S(1)}) custom-call(bf16[256,4096]{1,0:T(8,128)(2,1)S(1)} %bitcast.24, bf16[800,640]{1,0:T(8,128)(2,1)S(1)} %copy-done.3, bf16[800,640]{1,0:T(8,128)(2,1)} %collective-permute-done.other_ref, f32[1280,896]{1,0:T(8,128)} %shard_map.49.refs_0_.total_ref), custom_call_target="tpu_custom_call" | custom-call | flops 5242880000 | bytes 10240000 | tf_op jit(solution)/shard_map/pallas_call | solution.py:304
  113.8 3.2 %collective-permute-start.1 = (f32[7,640,128]{2,1,0:T(8,128)S(1)}, f32[7,640,128]{2,1,0:T(8,128)S(1)}, u32[]{:S(2)}, u32[]{:S(2)}) collective-permute-start(f32[7,640,128]{2,1,0:T(8,128)S(1)} %get-tuple-element.16), channel_id=1, source_target_pairs={{0,1},{1,0},{2,3},{3,2},{4,5},{5,4},{6,7},{7,6},{8,9},{9,8},{10,11... | collective-permute-start | bytes 6881288 | tf_op jit(solution)/shard_map/ppermute | solution.py:414
  116.9 0.0 slice-done
  116.9 0.0 slice-done.1
  116.9 2.2 %shard_map.51.keep_ref = f32[7,640,128]{2,1,0:T(8,128)S(1)} custom-call(bf16[640,1280]{1,0:T(8,128)(2,1)S(1)} %get-tuple-element.14.zed_ref, bf16[1280,800]{1,0:T(8,128)(2,1)S(1)} %get-tuple-element.15.rows_ref, f32[1280,896]{1,0:T(8,128)S(1)} %bitcast.23), custom_call_target="tpu_custom_call" | custom-call | flops 1468006400 | bytes 7864320 | tf_op jit(solution)/shard_map/pallas_call | solution.py:341
  119.1 1.9 %collective-permute-done.1.other_ref = f32[7,640,128]{2,1,0:T(8,128)S(1)} collective-permute-done((f32[7,640,128]{2,1,0:T(8,128)S(1)}, f32[7,640,128]{2,1,0:T(8,128)S(1)}, u32[]{:S(2)}, u32[]{:S(2)}) %collective-permute-start.1) | collective-permute-done | bytes 2293792 | tf_op jit(solution)/shard_map/ppermute | solution.py:414
  121.0 3.3 %shard_map.52 = bf16[32,5,4,800]{3,2,1,0:T(4,128)(2,1)} custom-call(f32[7,640,128]{2,1,0:T(8,128)S(1)} %shard_map.51.keep_ref, f32[7,640,128]{2,1,0:T(8,128)S(1)} %collective-permute-done.1.other_ref), custom_call_target="tpu_custom_call" | custom-call | tf_op jit(solution)/shard_map/pallas_call | solution.py:375
  124.3 4.4 %all-to-all-start.2 = ((bf16[32,5,4,800]{3,2,1,0:T(4,128)(2,1)}), bf16[32,5,4,800]{3,2,1,0:T(4,128)(2,1)S(1)}, u32[]{:S(2)}, u32[]{:S(2)}) async-start(bf16[32,5,4,800]{3,2,1,0:T(4,128)(2,1)} %shard_map.52), calls=%async_computation.2 | async-start | bytes 2293760 | tf_op jit(solution)/shard_map/all_to_all | solution.py:27
  128.7 0.1 slice_bitcast_fusion
  128.8 0.1 slice.13
  128.9 0.1 reshape.71
  129.0 0.1 reshape.70
  129.2 0.0 copy-start.5
  129.2 0.0 copy-start.6
  129.2 0.0 copy-start.4
  129.2 4.0 %fusion.1 = f32[8,5,800]{2,0,1:T(8,128)S(1)} fusion(bf16[5,800,640]{2,1,0:T(8,128)(2,1)} %param.5, bf16[8,256]{1,0:T(8,128)(2,1)S(1)} %reshape.71, bf16[8,384]{1,0:T(8,128)(2,1)S(1)} %reshape.70), kind=kOutput, calls=%fused_computation.8 | convolution fusion | flops 40980480 | bytes 5258240 | tf_op jit(solution)/shard_map/iap,rp->ria/dot_general | solution.py:430
  133.2 0.7 collective-permute-start.2
  134.0 12.8 %all-to-all-done.2 = bf16[32,5,4,800]{3,2,1,0:T(4,128)(2,1)S(1)} async-done(((bf16[32,5,4,800]{3,2,1,0:T(4,128)(2,1)}), bf16[32,5,4,800]{3,2,1,0:T(4,128)(2,1)S(1)}, u32[]{:S(2)}, u32[]{:S(2)}) %all-to-all-start.2) | async-done | bytes 1024032 | tf_op jit(solution)/shard_map/all_to_all | solution.py:27
  146.7 0.5 convert_reduce_fusion
  147.2 0.0 collective-permute-done.2
  147.3 2.5 %collective-permute-start.3 = (f32[4,5,800]{2,0,1:T(4,128)S(1)}, f32[4,5,800]{2,0,1:T(4,128)S(1)}, u32[]{:S(2)}, u32[]{:S(2)}) collective-permute-start(f32[4,5,800]{2,0,1:T(4,128)S(1)} %bitcast_subtract_fusion), channel_id=1, source_target_pairs={{0,2},{2,0},{1,3},{3,1},{4,6},{6,4},{5,7},{7,5},{8,10},{10,8},{9,1... | collective-permute-start | bytes 192008 | tf_op jit(solution)/shard_map/ppermute | solution.py:436
  149.8 2.2 %collective-permute-done.3 = f32[4,5,800]{2,0,1:T(4,128)S(1)} collective-permute-done((f32[4,5,800]{2,0,1:T(4,128)S(1)}, f32[4,5,800]{2,0,1:T(4,128)S(1)}, u32[]{:S(2)}, u32[]{:S(2)}) %collective-permute-start.3) | collective-permute-done | bytes 64032 | tf_op jit(solution)/shard_map/ppermute | solution.py:436
  152.1 3.0 %collective-permute-start.4 = (f32[4,5,800]{2,0,1:T(4,128)S(1)}, f32[4,5,800]{2,0,1:T(4,128)S(1)}, u32[]{:S(2)}, u32[]{:S(2)}) collective-permute-start(f32[4,5,800]{2,0,1:T(4,128)S(1)} %add.20), channel_id=1, source_target_pairs={{0,1},{1,0},{2,3},{3,2},{4,5},{5,4},{6,7},{7,6},{8,9},{9,8},{10,11... | collective-permute-start | bytes 192008 | tf_op jit(solution)/shard_map/ppermute | solution.py:437
  155.1 0.0 copy-done.5
  155.1 0.0 copy-done.6
  155.1 0.1 broadcast_subtract_fusion
  155.2 0.8 collective-permute-done.4
  156.0 0.0 copy-done.4
  156.0 0.7 fusion
  (8 shorter events, 0.1 us)
Async XLA Ops:
  10.3 60.4 %copy-start.1 = (bf16[256,4096]{1,0:T(8,128)(2,1)}, bf16[256,4096]{1,0:T(8,128)(2,1)S(1)}, u32[]{:S(2)}) copy-start(bf16[256,4096]{1,0:T(8,128)(2,1)S(1)} %get-tuple-element.13.send_ref) | copy-start | bytes 6291460
  72.7 31.3 %all-to-all-start.1 = ((bf16[32,8,4096]{2,1,0:T(8,128)(2,1)}), bf16[32,8,4096]{2,1,0:T(8,128)(2,1)S(1)}, u32[]{:S(2)}, u32[]{:S(2)}) async-start(bf16[32,8,4096]{2,1,0:T(8,128)(2,1)} %bitcast.21), calls=%async_computation.1 | async-start | bytes 4194304 | tf_op jit(solution)/shard_map/all_to_all | solution.py:27
  76.7 2.2 %copy-start = (bf16[32,16,4096]{2,1,0:T(8,128)(2,1)S(1)}, bf16[32,16,4096]{2,1,0:T(8,128)(2,1)}, u32[]{:S(2)}) copy-start(bf16[32,16,4096]{2,1,0:T(8,128)(2,1)} %all_to_all.15) | copy-start | bytes 12582916
  80.2 4.7 %copy-start.2 = (bf16[800,640]{1,0:T(8,128)(2,1)}, bf16[800,640]{1,0:T(8,128)(2,1)S(1)}, u32[]{:S(2)}) copy-start(bf16[800,640]{1,0:T(8,128)(2,1)S(1)} %shard_map.48.mine_ref) | copy-start | bytes 3072004
  80.3 4.7 %collective-permute-start = (bf16[800,640]{1,0:T(8,128)(2,1)S(1)}, bf16[800,640]{1,0:T(8,128)(2,1)}, u32[]{:S(2)}, u32[]{:S(2)}) collective-permute-start(bf16[800,640]{1,0:T(8,128)(2,1)S(1)} %shard_map.48.mine_ref), channel_id=1, source_target_pairs={{0,1},{1,0},{2,3},{3,2},{4,5},{5,4},{6,7},{7,6},{8,9},{9,8},{10,11... | collective-permute-start | bytes 3072008 | tf_op jit(solution)/shard_map/ppermute | solution.py:406
  103.9 13.0 %slice-start = ((s8[4587520]{0:T(1024)(128)(4,1)}), s8[4194304]{0:T(1024)(128)(4,1)S(1)}, s32[]{:S(2)}) async-start(s8[4587520]{0:T(1024)(128)(4,1)} %bitcast.22), calls=%async_computation.3 | async-start | bytes 8388608
  103.9 1.4 copy-start.3
  105.3 11.6 %slice-start.1 = ((s8[4587520]{0:T(1024)(128)(4,1)}), s8[393216]{0:T(1024)(128)(4,1)S(1)}, s32[]{:S(2)}) async-start(s8[4587520]{0:T(1024)(128)(4,1)} %bitcast.22), calls=%async_computation.4 | async-start | bytes 786432
  113.8 7.2 %collective-permute-start.1 = (f32[7,640,128]{2,1,0:T(8,128)S(1)}, f32[7,640,128]{2,1,0:T(8,128)S(1)}, u32[]{:S(2)}, u32[]{:S(2)}) collective-permute-start(f32[7,640,128]{2,1,0:T(8,128)S(1)} %get-tuple-element.16), channel_id=1, source_target_pairs={{0,1},{1,0},{2,3},{3,2},{4,5},{5,4},{6,7},{7,6},{8,9},{9,8},{10,11... | collective-permute-start | bytes 6881288 | tf_op jit(solution)/shard_map/ppermute | solution.py:414
  124.3 22.4 %all-to-all-start.2 = ((bf16[32,5,4,800]{3,2,1,0:T(4,128)(2,1)}), bf16[32,5,4,800]{3,2,1,0:T(4,128)(2,1)S(1)}, u32[]{:S(2)}, u32[]{:S(2)}) async-start(bf16[32,5,4,800]{3,2,1,0:T(4,128)(2,1)} %shard_map.52), calls=%async_computation.2 | async-start | bytes 2293760 | tf_op jit(solution)/shard_map/all_to_all | solution.py:27
  129.2 25.9 %copy-start.5 = (f32[800]{0:T(1024)S(1)}, f32[800]{0:T(1024)}, u32[]{:S(2)}) copy-start(f32[800]{0:T(1024)} %param.7) | copy-start | bytes 9604
  129.2 25.9 %copy-start.6 = (f32[5]{0:T(128)S(1)}, f32[5]{0:T(128)}, u32[]{:S(2)}) copy-start(f32[5]{0:T(128)} %param.6) | copy-start | bytes 64
  129.2 26.8 %copy-start.4 = (bf16[8,5,800]{2,0,1:T(8,128)(2,1)S(1)}, bf16[8,5,800]{2,0,1:T(8,128)(2,1)}, u32[]{:S(2)}) copy-start(bf16[8,5,800]{2,0,1:T(8,128)(2,1)} %param.4) | copy-start | bytes 192004
  133.2 14.0 %collective-permute-start.2 = (f32[4,5,800]{2,0,1:T(4,128)S(1)}, f32[4,5,800]{2,0,1:T(4,128)S(1)}, u32[]{:S(2)}, u32[]{:S(2)}) collective-permute-start(f32[4,5,800]{2,0,1:T(4,128)S(1)} %constant_dynamic-slice_fusion), channel_id=1, source_target_pairs={{0,1},{1,0},{2,3},{3,2},{4,5},{5,4},{6,7},{7,6},{8,9},{9,8},{10,11... | collective-permute-start | bytes 192008 | tf_op jit(solution)/shard_map/ppermute | solution.py:433
  147.3 4.8 %collective-permute-start.3 = (f32[4,5,800]{2,0,1:T(4,128)S(1)}, f32[4,5,800]{2,0,1:T(4,128)S(1)}, u32[]{:S(2)}, u32[]{:S(2)}) collective-permute-start(f32[4,5,800]{2,0,1:T(4,128)S(1)} %bitcast_subtract_fusion), channel_id=1, source_target_pairs={{0,2},{2,0},{1,3},{3,1},{4,6},{6,4},{5,7},{7,5},{8,10},{10,8},{9,1... | collective-permute-start | bytes 192008 | tf_op jit(solution)/shard_map/ppermute | solution.py:436
  152.1 3.9 %collective-permute-start.4 = (f32[4,5,800]{2,0,1:T(4,128)S(1)}, f32[4,5,800]{2,0,1:T(4,128)S(1)}, u32[]{:S(2)}, u32[]{:S(2)}) collective-permute-start(f32[4,5,800]{2,0,1:T(4,128)S(1)} %add.20), channel_id=1, source_target_pairs={{0,1},{1,0},{2,3},{3,2},{4,5},{5,4},{6,7},{7,6},{8,9},{9,8},{10,11... | collective-permute-start | bytes 192008 | tf_op jit(solution)/shard_map/ppermute | solution.py:437

commit v4 on v3

--- a/solution.py
+++ b/solution.py
@@ -14,12 +14,12 @@
 FIRST = 12
 CHUNK = 1024
 VMEM = pl.BlockSpec(memory_space=pltpu.VMEM)
-HBM = pl.BlockSpec(memory_space=pl.ANY)
+ANY = pl.BlockSpec(memory_space=pl.ANY)
 MIB = 1024 * 1024
 HIGH = 48 * MIB
 VLIM1 = 60 * MIB
-VLIM2 = 40 * MIB
-VLIM3 = 16 * MIB
+VLIM2 = 44 * MIB
+VLIM3 = 20 * MIB
 NT = (((1,), (1,)), ((), ()))
 
 
@@ -44,7 +44,7 @@
 
 
 def pack_kernel(
-    dims, core_ref, factors_ref, left_ref, first_ref, second_ref, sums, pick, lay, keep
+    dims, core_ref, factors_ref, left_ref, first_ref, second_ref, sums, pick, lay, keep, flat
 ):
     ranks, share, rows, roots = dims
     half = roots // 2
@@ -57,7 +57,7 @@
 
     def some(size):
         block = factors_ref[:size, :]
-        left = left_ref[:, :size]
+        left = flat[:, pl.ds(pl.multiple_of(k * CHUNK, CHUNK), size)]
         moved = lax.dot_general(pick[...], block[:, :cut], NT, preferred_element_type=jnp.float32)
         first_ref[:, :size] = (moved + dot(lay[...], left)).astype(jnp.bfloat16)
         moved = lax.dot_general(keep[...], block[:, cut:], NT, preferred_element_type=jnp.float32)
@@ -71,6 +71,9 @@
         row, col = iota((ranks * pitch, roots), 0), iota((ranks * pitch, roots), 1)
         at = row % pitch - FIRST
         lay[...] = one_hot((at >= 0) & (at + core_ref[0] * half == col))
+        for i in range(left_ref.shape[0]):
+            vir = left_ref.shape[2]
+            flat[:, i * vir : (i + 1) * vir] = left_ref[i]
         keep[...] = one_hot(iota((aux - cut, aux - cut), 0) == iota((aux - cut, aux - cut), 1))
         sums[...] = some(CHUNK)
 
@@ -111,7 +114,7 @@
         in_specs=[
             pl.BlockSpec(memory_space=pltpu.SMEM),
             pl.BlockSpec((CHUNK, ranks * share), lambda k: (k, 0)),
-            pl.BlockSpec((roots, CHUNK), lambda k: (0, k)),
+            VMEM,
         ],
         out_specs=[
             pl.BlockSpec((ranks * pitch, CHUNK), lambda k: (0, k)),
@@ -126,6 +129,7 @@
             pltpu.VMEM((ranks * pitch, ranks * FIRST), jnp.bfloat16),
             pltpu.VMEM((ranks * pitch, roots), jnp.bfloat16),
             pltpu.VMEM((ranks * rest, ranks * rest), jnp.bfloat16),
+            pltpu.VMEM((roots, steps * CHUNK), jnp.bfloat16),
         ],
         compiler_params=pltpu.CompilerParams(vmem_limit_bytes=HIGH),
     )(core, factors, lefts)
@@ -191,27 +195,62 @@
     )(got)
 
 
-def to_tiles(value, out_ref):
-    vir = value.shape[1]
-    for t in range(out_ref.shape[0]):
-        size = min(LANES, vir - t * LANES)
-        out_ref[t, :, :size] = value[:, t * LANES : t * LANES + size]
-
-
-def fetch_old(total_ref, old, sems):
-    rows = old.shape[0]
-    return pltpu.make_async_copy(total_ref.at[rows : 2 * rows, :], old, sems.at[4])
-
-
-def slab_kernel(dims, final, recv_ref, mine_ref, other_ref, *refs):
-    ranks, share, pitch, occ_local, vir, roots = dims
-    if final:
-        total_ref, give_ref, zed_ref, rows_e, left, sems, rows_z, zed, old = refs
-    else:
-        out_ref, left, sems, rows_z, rows_e, zed = refs
+def turn_rows(dims, recv_ref, rows_z, rows_e):
+    ranks, share, pitch, occ_local, vir, _ = dims
+    occ = ranks * occ_local
+    main = occ - ranks
+    group = min(ranks, 256 // pitch)
+    piece = group * pitch
+    row, col = iota((group * share, piece), 0), iota((group * share, piece), 1)
+    turn = one_hot(col == (row % group) * pitch + row // group)
+    for at in range(ranks // group):
+        for i in range(occ_local):
+            part = recv_ref[at * piece : (at + 1) * piece, i * vir : (i + 1) * vir]
+            part = dot(turn, part).astype(jnp.bfloat16)
+            for s in range(share):
+                rows = part[s * group : (s + 1) * group]
+                to = s * occ + i * ranks + at * group
+                rows_z[to : to + group, :] = rows
+                if i < occ_local - 1:
+                    to = s * main + i * ranks + at * group
+                else:
+                    to = share * main + s * ranks + at * group
+                rows_e[to : to + group, :] = rows
+
+
+def fill_zed(dims, rows_z, left, zed):
+    ranks, share, _, occ_local, _, roots = dims
     occ = ranks * occ_local
     main = occ - ranks
     packed = main // ranks
+    place = iota((occ, main), 1) // ranks
+
+    def some_vectors(k, carry):
+        at = pl.multiple_of(k * packed * occ, packed * occ)
+        z = dot(rows_z[pl.ds(at, packed * occ), :], left[...]).astype(jnp.bfloat16)
+        for r in range(roots):
+            low = roots * main + (r // packed) * main
+            rest = jnp.zeros((occ, main), jnp.bfloat16)
+            for s in range(packed):
+                zs = z[s * occ : (s + 1) * occ]
+                to = pl.multiple_of(k * packed * main, packed * main) + s * main
+                zed[r * occ : (r + 1) * occ, pl.ds(to, main)] = zs[:, r * main : (r + 1) * main]
+                turned = zs[:, low : low + main]
+                shift = (s - r % packed) % packed * ranks
+                if shift:
+                    turned = pltpu.roll(turned, shift, 1)
+                rest = jnp.where(place == s, turned, rest)
+            to = pl.multiple_of(share * main + k * main, main)
+            zed[r * occ : (r + 1) * occ, pl.ds(to, main)] = rest
+        return carry
+
+    lax.fori_loop(0, share // packed, some_vectors, 0)
+
+
+def slab_kernel(dims, recv_ref, mine_ref, other_ref, out_ref, left, sems, rows_z, rows_e, zed):
+    ranks, _, _, occ_local, vir, roots = dims
+    occ = ranks * occ_local
+    main = occ - ranks
     half = roots // 2
 
     @pl.when(pl.program_id(0) == 0)
@@ -231,130 +270,88 @@
                 )
         for copy in copies:
             copy.start()
-        if final:
-            fetch_old(total_ref, old, sems).start()
-
-        group = min(ranks, 256 // pitch)
-        piece = group * pitch
-        row, col = iota((group * share, piece), 0), iota((group * share, piece), 1)
-        turn = one_hot(col == (row % group) * pitch + row // group)
-        for at in range(ranks // group):
-            for i in range(occ_local):
-                part = recv_ref[at * piece : (at + 1) * piece, i * vir : (i + 1) * vir]
-                part = dot(turn, part).astype(jnp.bfloat16)
-                for s in range(share):
-                    rows = part[s * group : (s + 1) * group]
-                    to = s * occ + i * ranks + at * group
-                    rows_z[to : to + group, :] = rows
-                    if i < occ_local - 1:
-                        to = s * main + i * ranks + at * group
-                    else:
-                        to = share * main + s * ranks + at * group
-                    rows_e[to : to + group, :] = rows
-
+        turn_rows(dims, recv_ref, rows_z, rows_e)
         for copy in copies:
             copy.wait()
-        place = iota((occ, main), 1) // ranks
-
-        def put(r, to, value):
-            if final and r < half:
-                zed_ref[r * occ : (r + 1) * occ, pl.ds(to, main)] = value
-            else:
-                at = r - half if final else r
-                zed[at * occ : (at + 1) * occ, pl.ds(to, main)] = value
-
-        def some_vectors(k, carry):
-            at = pl.multiple_of(k * packed * occ, packed * occ)
-            z = dot(rows_z[pl.ds(at, packed * occ), :], left[...]).astype(jnp.bfloat16)
-            for r in range(roots):
-                low = roots * main + (r // packed) * main
-                rest = jnp.zeros((occ, main), jnp.bfloat16)
-                for s in range(packed):
-                    zs = z[s * occ : (s + 1) * occ]
-                    to = pl.multiple_of(k * packed * main, packed * main) + s * main
-                    put(r, to, zs[:, r * main : (r + 1) * main])
-                    turned = zs[:, low : low + main]
-                    shift = (s - r % packed) % packed * ranks
-                    if shift:
-                        turned = pltpu.roll(turned, shift, 1)
-                    rest = jnp.where(place == s, turned, rest)
-                put(r, pl.multiple_of(share * main + k * main, main), rest)
-            return carry
-
-        lax.fori_loop(0, share // packed, some_vectors, 0)
-
-    if final:
-        part = dot(zed[...], rows_e[...])
-        fetch_old(total_ref, old, sems).wait()
-        to_tiles(old[:, :vir] + part, give_ref)
-    else:
-        step = out_ref.shape[0]
-        at = pl.multiple_of(pl.program_id(0) * step, step)
-        out_ref[:, :vir] = dot(zed[pl.ds(at, step), :], rows_e[...])
-
-
-def slab_product(recv, mine, other, total, dims):
+        fill_zed(dims, rows_z, left, zed)
+
+    step = out_ref.shape[0]
+    at = pl.multiple_of(pl.program_id(0) * step, step)
+    out_ref[:, :vir] = dot(zed[pl.ds(at, step), :], rows_e[...])
+
+
+def slab_product(recv, mine, other, dims):
     ranks, share, _, occ_local, vir, roots = dims
     occ = ranks * occ_local
     width = up(vir, LANES)
-    final = total is not None
-    steps = 1 if final else 4
-    rows = roots * occ // (2 if final else 4)
-    args = [recv, mine, other] + ([total] if final else [])
-    return pl.pallas_call(
-        functools.partial(slab_kernel, dims, final),
+    steps = 4
+    rows = roots * occ // steps
+    return pl.pallas_call(
+        functools.partial(slab_kernel, dims),
         grid=(steps,),
-        in_specs=[VMEM, HBM, HBM] + ([HBM] if final else []),
-        out_specs=[VMEM, VMEM, VMEM] if final else pl.BlockSpec((rows, width), lambda k: (k, 0)),
-        out_shape=[
-            jax.ShapeDtypeStruct((width // LANES, rows, LANES), jnp.float32),
-            jax.ShapeDtypeStruct((rows, share * occ), jnp.bfloat16),
-            jax.ShapeDtypeStruct((share * occ, vir), jnp.bfloat16),
-        ]
-        if final
-        else jax.ShapeDtypeStruct((roots * occ, width), jnp.float32),
+        in_specs=[VMEM, ANY, ANY],
+        out_specs=pl.BlockSpec((rows, width), lambda k: (k, 0)),
+        out_shape=jax.ShapeDtypeStruct((roots * occ, width), jnp.float32),
         scratch_shapes=[
             pltpu.VMEM((vir, roots * occ), jnp.bfloat16),
-            pltpu.SemaphoreType.DMA((5,)),
+            pltpu.SemaphoreType.DMA((4,)),
             pltpu.VMEM((share * occ, vir), jnp.bfloat16),
-        ]
-        + ([] if final else [pltpu.VMEM((share * occ, vir), jnp.bfloat16)])
-        + [pltpu.VMEM((rows if final else roots * occ, share * occ), jnp.bfloat16)]
-        + ([pltpu.VMEM((rows, width), jnp.float32)] if final else []),
-        compiler_params=pltpu.CompilerParams(vmem_limit_bytes=VLIM2 if final else VLIM1),
+            pltpu.VMEM((share * occ, vir), jnp.bfloat16),
+            pltpu.VMEM((roots * occ, share * occ), jnp.bfloat16),
+        ],
+        compiler_params=pltpu.CompilerParams(vmem_limit_bytes=VLIM1),
         cost_estimate=pl.CostEstimate(
             flops=4 * share * occ * roots * occ * vir,
             transcendentals=0,
             bytes_accessed=2 * share * occ * vir + 8 * roots * occ * vir,
         ),
-    )(*args)
-
-
-def keep_kernel(zed_ref, rows_ref, total_ref, out_ref):
-    vir = rows_ref.shape[1]
-    to_tiles(total_ref[:, :vir] + dot(zed_ref[...], rows_ref[...]), out_ref)
-
-
-def keep_product(zed, rows_e, total):
-    rows, width = zed.shape[0], total.shape[1]
-    step = rows // 2
-    return pl.pallas_call(
-        keep_kernel,
-        grid=(2,),
-        in_specs=[
-            pl.BlockSpec((step, zed.shape[1]), lambda k: (k, 0)),
-            VMEM,
-            pl.BlockSpec((step, width), lambda k: (k, 0)),
-        ],
-        out_specs=pl.BlockSpec((width // LANES, step, LANES), lambda k: (0, k, 0)),
-        out_shape=jax.ShapeDtypeStruct((width // LANES, rows, LANES), jnp.float32),
-        compiler_params=pltpu.CompilerParams(vmem_limit_bytes=VLIM3),
+    )(recv, mine, other)
+
+
+def half_kernel(dims, place, *refs):
+    vir = dims[4]
+    if place:
+        recv_ref, left_ref, total_ref, out_ref, rows_z, rows_e, zed, old, sem = refs
+    else:
+        rows_z, rows_e, left_ref, total_ref, out_ref, zed, old, sem = refs
+    rows = old.shape[0]
+    fetch = pltpu.make_async_copy(total_ref.at[place * rows : (place + 1) * rows, :], old, sem)
+    fetch.start()
+    if place:
+        turn_rows(dims, recv_ref, rows_z, rows_e)
+    fill_zed(dims, rows_z, left_ref, zed)
+    part = dot(zed[...], rows_e[...])
+    fetch.wait()
+    for t in range(out_ref.shape[0]):
+        at = t * LANES
+        size = min(LANES, vir - at)
+        out_ref[t, :, :size] = old[:, at : at + size] + part[:, at : at + size]
+
+
+def half_product(args, place, total, dims):
+    ranks, share, _, occ_local, vir, roots = dims
+    occ = ranks * occ_local
+    rows = roots * occ
+    width = up(vir, LANES)
+    made = [jax.ShapeDtypeStruct((share * occ, vir), jnp.bfloat16)] * 2
+    return pl.pallas_call(
+        functools.partial(half_kernel, dims, place),
+        in_specs=[VMEM] * len(args) + [ANY],
+        out_specs=[VMEM] * (3 if place else 1),
+        out_shape=[jax.ShapeDtypeStruct((width // LANES, rows, LANES), jnp.float32)]
+        + (made if place else []),
+        scratch_shapes=[
+            pltpu.VMEM((rows, share * occ), jnp.bfloat16),
+            pltpu.VMEM((rows, width), jnp.float32),
+            pltpu.SemaphoreType.DMA,
+        ],
+        compiler_params=pltpu.CompilerParams(vmem_limit_bytes=VLIM2 if place else VLIM3),
         cost_estimate=pl.CostEstimate(
-            flops=2 * rows * zed.shape[1] * width,
+            flops=4 * share * occ * rows * vir,
             transcendentals=0,
-            bytes_accessed=8 * rows * width + 4 * rows * zed.shape[1],
+            bytes_accessed=2 * share * occ * vir + 8 * rows * vir,
         ),
-    )(zed, rows_e, total)
+    )(*args, total)
 
 
 def merge_kernel(keep_ref, other_ref, out_ref, tiles):
@@ -393,9 +390,11 @@
     core = lax.rem(lax.axis_index("chol"), 2)
     dims = (ranks, share, rows, roots)
 
-    lefts = jnp.pad(left_vectors.reshape(roots, rows), ((0, 0), (0, up(rows, CHUNK) - rows)))
     first_send, second_send = pack(
-        chol_factors.reshape(rows, aux_local), lefts, core.reshape(1), dims
+        chol_factors.reshape(rows, aux_local),
+        left_vectors.transpose(1, 0, 2),
+        core.reshape(1),
+        dims,
     )
 
     pitch = FIRST + half
@@ -405,14 +404,11 @@
     mine = left_half(first, (ranks, occ_local, vir, half))
     other = lax.ppermute(mine, "chol", CORE_SWAP)
 
-    total = slab_product(
-        first, mine, other, None, (ranks, FIRST, pitch, occ_local, vir, roots)
-    )
-    give, zed, rows_e = slab_product(
-        second, mine, other, total, (ranks, rest, rest, occ_local, vir, roots)
-    )
+    total = slab_product(first, mine, other, (ranks, FIRST, pitch, occ_local, vir, roots))
+    last = (ranks, rest, rest, occ_local, vir, half)
+    give, rows_z, rows_e = half_product([second, other], 1, total, last)
     got = lax.ppermute(give, "chol", CORE_SWAP)
-    keep = keep_product(zed, rows_e, total)
+    (keep,) = half_product([rows_z, rows_e, mine], 0, total, last)
 
     merged = merge(keep, got, (ranks, occ_local, half, vir))
     merged, second = lax.optimization_barrier((merged, second))

time: 157 us -> 156 us (level)
  Pallas kernels: 44.6 us -> 46.4 us
    ppermute x1, waiting for transfers between devices: 1.87 us -> 0.01 us  [body(): got = lax.ppermute(give, 'chol', CORE_SWAP)]
    pallas_call x3, Pallas kernels: 28.7 us -> 30.4 us  [the longest x1 18 us: slab_product(): pl.pallas_call(functools.partial(slab_kernel, dims), grid=(steps,), in_sp...]
    unnamed x19 -> x20, local copies, waits for them, and re-layouts: 4.48 us -> 3.1 us
  transfers between devices with their start and end apart: 7 -> 7, of which waited for: 6 -> 5; matrix products, arithmetic and copies ran while one was open for 3% -> 3% of each run, Pallas kernels for 14% -> 16%
where the time goes in v4:
time: 156 us; the launch traced here: 155 us
  blocking collectives  60.4 us (39%)
  Pallas kernels  46.4 us (30%)
  starting transfers between devices  20 us (13%)
  waiting for transfers between devices  19.6 us (13%)
  matrix products  3.99 us (3%)
  local copies, waits for them, and re-layouts  3.59 us (2%)
    all_to_all x1, blocking collectives, exchange(): lax.all_to_all(blocks, 'pair', split_axis=0, concat_axis=0, tiled=True)  60.4 us
    pallas_call x1, Pallas kernels, slab_product(): pl.pallas_call(functools.partial(slab_kernel, dims), grid=(steps,), in_sp...  18 us
    all_to_all x2, waiting for transfers between devices, exchange(): lax.all_to_all(blocks, 'pair', split_axis=0, concat_axis=0, tiled=True)  14.2 us
    pallas_call x2, Pallas kernels, half_product(): pl.pallas_call(functools.partial(half_kernel, dims, place), in_specs=[VME...  12.3 us
    pallas_call x1, Pallas kernels, pack(): pl.pallas_call(functools.partial(pack_kernel, dims), grid=(steps,), in_sp...  9.36 us
    all_to_all x2, starting transfers between devices, exchange(): lax.all_to_all(blocks, 'pair', split_axis=0, concat_axis=0, tiled=True)  8.43 us
    dot_general x1, matrix products, body(): jnp.einsum('iap,rp->ria', chol_factors, coul_vec, preferred_element_type=...  3.99 us
    ppermute x1, starting transfers between devices, body(): got = lax.ppermute(give, 'chol', CORE_SWAP)  3.39 us
  transfers between devices with their start and end apart: 7, of which 5 were waited for; matrix products, arithmetic and copies ran while one was open for 3% of the time, Pallas kernels for 16%

profile of v4, /device:TPU:1, one launch (start us, length us, event | category | flops | bytes accessed | tf_op | source)
XLA Modules:
  0.0 155.4 jit_solution(9052583965865075055)
XLA Ops:
  0.0 0.0 copy-start.4
  0.0 0.9 copy-done.4
  0.9 9.4 %shard_map.46 = (bf16[512,4096]{1,0:T(8,128)(2,1)}, bf16[256,4096]{1,0:T(8,128)(2,1)S(1)}) custom-call(s32[1]{0:T(128)} %bitcast.core_ref, bf16[4000,640]{1,0:T(8,128)(2,1)} %bitcast.28, bf16[5,8,800]{2,1,0:T(8,128)(2,1)S(1)} %bitcast.27), custom_call_target="tpu_custom_call" | custom-call | tf_op jit(solution)/shard_map/pallas_call | solution.py:111
  10.2 0.0 copy-start.1
  10.2 60.4 %all_to_all.15 = bf16[32,16,4096]{2,1,0:T(8,128)(2,1)} all-to-all(bf16[32,16,4096]{2,1,0:T(8,128)(2,1)} %bitcast.29), channel_id=1, replica_groups=mesh['pair'=32,'chol'=4] {'pair'}, dimensions={0} | all-to-all | bytes 8388608 | tf_op jit(solution)/shard_map/all_to_all | solution.py:27
  70.6 0.0 copy-done.1
  70.6 2.0 %shard_map.47 = bf16[256,4096]{1,0:T(8,128)(2,1)} custom-call(bf16[512,4096]{1,0:T(8,128)(2,1)} %bitcast.19, bf16[256,4096]{1,0:T(8,128)(2,1)} %copy-done.1), custom_call_target="tpu_custom_call", output_to_operand_aliasing={{}: (1, {})} | custom-call | tf_op jit(solution)/shard_map/pallas_call | solution.py:157
  72.6 4.0 %all-to-all-start.1 = ((bf16[32,8,4096]{2,1,0:T(8,128)(2,1)}), bf16[32,8,4096]{2,1,0:T(8,128)(2,1)S(1)}, u32[]{:S(2)}, u32[]{:S(2)}) async-start(bf16[32,8,4096]{2,1,0:T(8,128)(2,1)} %bitcast.22), calls=%async_computation.1 | async-start | bytes 4194304 | tf_op jit(solution)/shard_map/all_to_all | solution.py:27
  76.6 0.0 copy-start
  76.6 2.2 %copy-done = bf16[32,16,4096]{2,1,0:T(8,128)(2,1)S(1)} copy-done((bf16[32,16,4096]{2,1,0:T(8,128)(2,1)S(1)}, bf16[32,16,4096]{2,1,0:T(8,128)(2,1)}, u32[]{:S(2)}) %copy-start) | copy-done | bytes 4194328
  78.8 1.4 shard_map.48.mine_ref.refs_2_
  80.2 0.0 copy-start.2
  80.2 2.3 %collective-permute-start = (bf16[800,640]{1,0:T(8,128)(2,1)S(1)}, bf16[800,640]{1,0:T(8,128)(2,1)}, u32[]{:S(2)}, u32[]{:S(2)}) collective-permute-start(bf16[800,640]{1,0:T(8,128)(2,1)S(1)} %shard_map.48.mine_ref.refs_2_), channel_id=1, source_target_pairs={{0,1},{1,0},{2,3},{3,2},{4,5},{5,4},{6,7},{7,6},{8,9},{9,8},{10,11... | collective-permute-start | bytes 3072008 | tf_op jit(solution)/shard_map/ppermute | solution.py:405
  82.5 2.4 %collective-permute-done.other_ref.refs_1_ = bf16[800,640]{1,0:T(8,128)(2,1)} collective-permute-done((bf16[800,640]{1,0:T(8,128)(2,1)S(1)}, bf16[800,640]{1,0:T(8,128)(2,1)}, u32[]{:S(2)}, u32[]{:S(2)}) %collective-permute-start) | collective-permute-done | bytes 1024032 | tf_op jit(solution)/shard_map/ppermute | solution.py:405
  84.9 0.0 copy-done.2
  84.9 18.0 %shard_map.49.refs_2_.refs_3_ = f32[1280,896]{1,0:T(8,128)} custom-call(bf16[512,4096]{1,0:T(8,128)(2,1)} %bitcast.20, bf16[800,640]{1,0:T(8,128)(2,1)} %copy-done.2, bf16[800,640]{1,0:T(8,128)(2,1)} %collective-permute-done.other_ref.refs_1_), custom_call_target="tpu_custom_call" | custom-call | flops 7864320000 | bytes 11264000 | tf_op jit(solution)/shard_map/pallas_call | solution.py:289
  103.0 0.9 all-to-all-done.1
  103.9 0.0 slice-start
  103.9 7.1 %shard_map.50 = (f32[7,640,128]{2,1,0:T(8,128)S(1)}, bf16[1280,800]{1,0:T(8,128)(2,1)S(1)}, bf16[1280,800]{1,0:T(8,128)(2,1)S(1)}) custom-call(bf16[256,4096]{1,0:T(8,128)(2,1)S(1)} %bitcast.25, bf16[800,640]{1,0:T(8,128)(2,1)} %collective-permute-done.other_ref.refs_1_, f32[1280,896]{1,0:T(8,128)} %shard_map.49.refs_2_.refs_3_), custom_call_target="tpu_custom_call" | custom-call | flops 2621440000 | bytes 6144000 | tf_op jit(solution)/shard_map/pallas_call | solution.py:337
  111.0 3.4 %collective-permute-start.1 = (f32[7,640,128]{2,1,0:T(8,128)S(1)}, f32[7,640,128]{2,1,0:T(8,128)S(1)}, u32[]{:S(2)}, u32[]{:S(2)}) collective-permute-start(f32[7,640,128]{2,1,0:T(8,128)S(1)} %get-tuple-element.16), channel_id=1, source_target_pairs={{0,1},{1,0},{2,3},{3,2},{4,5},{5,4},{6,7},{7,6},{8,9},{9,8},{10,11... | collective-permute-start | bytes 6881288 | tf_op jit(solution)/shard_map/ppermute | solution.py:410
  114.3 0.0 slice-done
  114.3 0.0 slice-done.1
  114.3 0.0 copy-done.3
  114.4 5.2 %shard_map.51.keep_ref = f32[7,640,128]{2,1,0:T(8,128)S(1)} custom-call(bf16[1280,800]{1,0:T(8,128)(2,1)S(1)} %get-tuple-element.14.refs_0_, bf16[1280,800]{1,0:T(8,128)(2,1)S(1)} %get-tuple-element.15.refs_1_, bf16[800,640]{1,0:T(8,128)(2,1)S(1)} %copy-done.3, f32[1280,896]{1,0:T(8,128)S(1)} %bitcast.24), custom_call_target="tpu_custom_call" | custom-call | flops 2621440000 | bytes 6144000 | tf_op jit(solution)/shard_map/pallas_call | solution.py:337
  119.6 0.0 collective-permute-done.1.other_ref
  119.6 3.3 %shard_map.52 = bf16[32,5,4,800]{3,2,1,0:T(4,128)(2,1)} custom-call(f32[7,640,128]{2,1,0:T(8,128)S(1)} %shard_map.51.keep_ref, f32[7,640,128]{2,1,0:T(8,128)S(1)} %collective-permute-done.1.other_ref), custom_call_target="tpu_custom_call" | custom-call | tf_op jit(solution)/shard_map/pallas_call | solution.py:372
  123.0 4.4 %all-to-all-start.2 = ((bf16[32,5,4,800]{3,2,1,0:T(4,128)(2,1)}), bf16[32,5,4,800]{3,2,1,0:T(4,128)(2,1)S(1)}, u32[]{:S(2)}, u32[]{:S(2)}) async-start(bf16[32,5,4,800]{3,2,1,0:T(4,128)(2,1)} %shard_map.52), calls=%async_computation.2 | async-start | bytes 2293760 | tf_op jit(solution)/shard_map/all_to_all | solution.py:27
  127.4 0.1 slice_bitcast_fusion
  127.5 0.1 slice.13
  127.6 0.1 reshape.67
  127.7 0.1 reshape.66
  127.9 0.0 copy-start.6
  127.9 0.0 copy-start.7
  127.9 0.0 copy-start.5
  127.9 4.0 %fusion.1 = f32[8,5,800]{2,0,1:T(8,128)S(1)} fusion(bf16[5,800,640]{2,1,0:T(8,128)(2,1)} %param.5, bf16[8,256]{1,0:T(8,128)(2,1)S(1)} %reshape.67, bf16[8,384]{1,0:T(8,128)(2,1)S(1)} %reshape.66), kind=kOutput, calls=%fused_computation.8 | convolution fusion | flops 40980480 | bytes 5258240 | tf_op jit(solution)/shard_map/iap,rp->ria/dot_general | solution.py:426
  131.9 0.5 collective-permute-start.2
  132.4 13.2 %all-to-all-done.2 = bf16[32,5,4,800]{3,2,1,0:T(4,128)(2,1)S(1)} async-done(((bf16[32,5,4,800]{3,2,1,0:T(4,128)(2,1)}), bf16[32,5,4,800]{3,2,1,0:T(4,128)(2,1)S(1)}, u32[]{:S(2)}, u32[]{:S(2)}) %all-to-all-start.2) | async-done | bytes 1024032 | tf_op jit(solution)/shard_map/all_to_all | solution.py:27
  145.7 0.5 convert_reduce_fusion
  146.2 0.0 collective-permute-done.2
  146.2 2.5 %collective-permute-start.3 = (f32[4,5,800]{2,0,1:T(4,128)S(1)}, f32[4,5,800]{2,0,1:T(4,128)S(1)}, u32[]{:S(2)}, u32[]{:S(2)}) collective-permute-start(f32[4,5,800]{2,0,1:T(4,128)S(1)} %bitcast_subtract_fusion), channel_id=1, source_target_pairs={{0,2},{2,0},{1,3},{3,1},{4,6},{6,4},{5,7},{7,5},{8,10},{10,8},{9,1... | collective-permute-start | bytes 192008 | tf_op jit(solution)/shard_map/ppermute | solution.py:432
  148.7 2.2 %collective-permute-done.3 = f32[4,5,800]{2,0,1:T(4,128)S(1)} collective-permute-done((f32[4,5,800]{2,0,1:T(4,128)S(1)}, f32[4,5,800]{2,0,1:T(4,128)S(1)}, u32[]{:S(2)}, u32[]{:S(2)}) %collective-permute-start.3) | collective-permute-done | bytes 64032 | tf_op jit(solution)/shard_map/ppermute | solution.py:432
  151.0 2.8 %collective-permute-start.4 = (f32[4,5,800]{2,0,1:T(4,128)S(1)}, f32[4,5,800]{2,0,1:T(4,128)S(1)}, u32[]{:S(2)}, u32[]{:S(2)}) collective-permute-start(f32[4,5,800]{2,0,1:T(4,128)S(1)} %add.18), channel_id=1, source_target_pairs={{0,1},{1,0},{2,3},{3,2},{4,5},{5,4},{6,7},{7,6},{8,9},{9,8},{10,11... | collective-permute-start | bytes 192008 | tf_op jit(solution)/shard_map/ppermute | solution.py:433
  153.8 0.0 copy-done.6
  153.8 0.0 copy-done.7
  153.8 0.1 broadcast_subtract_fusion
  153.9 0.8 collective-permute-done.4
  154.7 0.0 copy-done.5
  154.7 0.7 fusion
  (7 shorter events, 0.1 us)
Async XLA Ops:
  0.0 0.9 copy-start.4
  10.2 60.4 %copy-start.1 = (bf16[256,4096]{1,0:T(8,128)(2,1)}, bf16[256,4096]{1,0:T(8,128)(2,1)S(1)}, u32[]{:S(2)}) copy-start(bf16[256,4096]{1,0:T(8,128)(2,1)S(1)} %get-tuple-element.13.send_ref) | copy-start | bytes 6291460
  72.6 31.3 %all-to-all-start.1 = ((bf16[32,8,4096]{2,1,0:T(8,128)(2,1)}), bf16[32,8,4096]{2,1,0:T(8,128)(2,1)S(1)}, u32[]{:S(2)}, u32[]{:S(2)}) async-start(bf16[32,8,4096]{2,1,0:T(8,128)(2,1)} %bitcast.22), calls=%async_computation.1 | async-start | bytes 4194304 | tf_op jit(solution)/shard_map/all_to_all | solution.py:27
  76.6 2.2 %copy-start = (bf16[32,16,4096]{2,1,0:T(8,128)(2,1)S(1)}, bf16[32,16,4096]{2,1,0:T(8,128)(2,1)}, u32[]{:S(2)}) copy-start(bf16[32,16,4096]{2,1,0:T(8,128)(2,1)} %all_to_all.15) | copy-start | bytes 12582916
  80.2 4.7 %copy-start.2 = (bf16[800,640]{1,0:T(8,128)(2,1)}, bf16[800,640]{1,0:T(8,128)(2,1)S(1)}, u32[]{:S(2)}) copy-start(bf16[800,640]{1,0:T(8,128)(2,1)S(1)} %shard_map.48.mine_ref.refs_2_) | copy-start | bytes 3072004
  80.2 4.7 %collective-permute-start = (bf16[800,640]{1,0:T(8,128)(2,1)S(1)}, bf16[800,640]{1,0:T(8,128)(2,1)}, u32[]{:S(2)}, u32[]{:S(2)}) collective-permute-start(bf16[800,640]{1,0:T(8,128)(2,1)S(1)} %shard_map.48.mine_ref.refs_2_), channel_id=1, source_target_pairs={{0,1},{1,0},{2,3},{3,2},{4,5},{5,4},{6,7},{7,6},{8,9},{9,8},{10,11... | collective-permute-start | bytes 3072008 | tf_op jit(solution)/shard_map/ppermute | solution.py:405
  103.9 10.5 %slice-start = ((s8[4587520]{0:T(1024)(128)(4,1)}), s8[4194304]{0:T(1024)(128)(4,1)S(1)}, s32[]{:S(2)}) async-start(s8[4587520]{0:T(1024)(128)(4,1)} %bitcast.23), calls=%async_computation.3 | async-start | bytes 8388608
  103.9 10.5 %slice-start.1 = ((s8[4587520]{0:T(1024)(128)(4,1)}), s8[393216]{0:T(1024)(128)(4,1)S(1)}, s32[]{:S(2)}) async-start(s8[4587520]{0:T(1024)(128)(4,1)} %bitcast.23), calls=%async_computation.4 | async-start | bytes 786432
  103.9 10.5 %copy-start.3 = (bf16[800,640]{1,0:T(8,128)(2,1)S(1)}, bf16[800,640]{1,0:T(8,128)(2,1)}, u32[]{:S(2)}) copy-start(bf16[800,640]{1,0:T(8,128)(2,1)} %copy-done.2) | copy-start | bytes 3072004
  111.0 8.7 %collective-permute-start.1 = (f32[7,640,128]{2,1,0:T(8,128)S(1)}, f32[7,640,128]{2,1,0:T(8,128)S(1)}, u32[]{:S(2)}, u32[]{:S(2)}) collective-permute-start(f32[7,640,128]{2,1,0:T(8,128)S(1)} %get-tuple-element.16), channel_id=1, source_target_pairs={{0,1},{1,0},{2,3},{3,2},{4,5},{5,4},{6,7},{7,6},{8,9},{9,8},{10,11... | collective-permute-start | bytes 6881288 | tf_op jit(solution)/shard_map/ppermute | solution.py:410
  123.0 22.7 %all-to-all-start.2 = ((bf16[32,5,4,800]{3,2,1,0:T(4,128)(2,1)}), bf16[32,5,4,800]{3,2,1,0:T(4,128)(2,1)S(1)}, u32[]{:S(2)}, u32[]{:S(2)}) async-start(bf16[32,5,4,800]{3,2,1,0:T(4,128)(2,1)} %shard_map.52), calls=%async_computation.2 | async-start | bytes 2293760 | tf_op jit(solution)/shard_map/all_to_all | solution.py:27
  127.9 25.9 %copy-start.6 = (f32[800]{0:T(1024)S(1)}, f32[800]{0:T(1024)}, u32[]{:S(2)}) copy-start(f32[800]{0:T(1024)} %param.7) | copy-start | bytes 9604
  127.9 25.9 %copy-start.7 = (f32[5]{0:T(128)S(1)}, f32[5]{0:T(128)}, u32[]{:S(2)}) copy-start(f32[5]{0:T(128)} %param.6) | copy-start | bytes 64
  127.9 26.8 %copy-start.5 = (bf16[8,5,800]{2,0,1:T(8,128)(2,1)S(1)}, bf16[8,5,800]{2,0,1:T(8,128)(2,1)}, u32[]{:S(2)}) copy-start(bf16[8,5,800]{2,0,1:T(8,128)(2,1)} %param.4) | copy-start | bytes 192004
  131.9 14.2 %collective-permute-start.2 = (f32[4,5,800]{2,0,1:T(4,128)S(1)}, f32[4,5,800]{2,0,1:T(4,128)S(1)}, u32[]{:S(2)}, u32[]{:S(2)}) collective-permute-start(f32[4,5,800]{2,0,1:T(4,128)S(1)} %constant_dynamic-slice_fusion), channel_id=1, source_target_pairs={{0,1},{1,0},{2,3},{3,2},{4,5},{5,4},{6,7},{7,6},{8,9},{9,8},{10,11... | collective-permute-start | bytes 192008 | tf_op jit(solution)/shard_map/ppermute | solution.py:429
  146.2 4.8 %collective-permute-start.3 = (f32[4,5,800]{2,0,1:T(4,128)S(1)}, f32[4,5,800]{2,0,1:T(4,128)S(1)}, u32[]{:S(2)}, u32[]{:S(2)}) collective-permute-start(f32[4,5,800]{2,0,1:T(4,128)S(1)} %bitcast_subtract_fusion), channel_id=1, source_target_pairs={{0,2},{2,0},{1,3},{3,1},{4,6},{6,4},{5,7},{7,5},{8,10},{10,8},{9,1... | collective-permute-start | bytes 192008 | tf_op jit(solution)/shard_map/ppermute | solution.py:432
  151.0 3.7 %collective-permute-start.4 = (f32[4,5,800]{2,0,1:T(4,128)S(1)}, f32[4,5,800]{2,0,1:T(4,128)S(1)}, u32[]{:S(2)}, u32[]{:S(2)}) collective-permute-start(f32[4,5,800]{2,0,1:T(4,128)S(1)} %add.18), channel_id=1, source_target_pairs={{0,1},{1,0},{2,3},{3,2},{4,5},{5,4},{6,7},{7,6},{8,9},{9,8},{10,11... | collective-permute-start | bytes 192008 | tf_op jit(solution)/shard_map/ppermute | solution.py:433

commit v5 on v4

--- a/solution.py
+++ b/solution.py
@@ -44,7 +44,7 @@
 
 
 def pack_kernel(
-    dims, core_ref, factors_ref, left_ref, first_ref, second_ref, sums, pick, lay, keep, flat
+    dims, core_ref, factors_ref, left_ref, first_ref, second_ref, sums, pick, flat, own
 ):
     ranks, share, rows, roots = dims
     half = roots // 2
@@ -59,22 +59,23 @@
         block = factors_ref[:size, :]
         left = flat[:, pl.ds(pl.multiple_of(k * CHUNK, CHUNK), size)]
         moved = lax.dot_general(pick[...], block[:, :cut], NT, preferred_element_type=jnp.float32)
-        first_ref[:, :size] = (moved + dot(lay[...], left)).astype(jnp.bfloat16)
-        moved = lax.dot_general(keep[...], block[:, cut:], NT, preferred_element_type=jnp.float32)
-        second_ref[:, :size] = moved.astype(jnp.bfloat16)
+        first_ref[:, :size] = moved.astype(jnp.bfloat16)
+        mine = own[:, pl.ds(pl.multiple_of(k * CHUNK, CHUNK), size)]
+        for d in range(ranks):
+            first_ref[d * pitch + FIRST : (d + 1) * pitch, :size] = mine
+        for at in range(0, size, LANES):
+            to = min(LANES, size - at)
+            second_ref[:, at : at + to] = block[at : at + to, cut:].T
         return dot(left, block)
 
     @pl.when(k == 0)
     def _():
         row, col = iota((ranks * pitch, cut), 0), iota((ranks * pitch, cut), 1)
         pick[...] = one_hot((row % pitch < FIRST) & (col == row // pitch * FIRST + row % pitch))
-        row, col = iota((ranks * pitch, roots), 0), iota((ranks * pitch, roots), 1)
-        at = row % pitch - FIRST
-        lay[...] = one_hot((at >= 0) & (at + core_ref[0] * half == col))
         for i in range(left_ref.shape[0]):
             vir = left_ref.shape[2]
             flat[:, i * vir : (i + 1) * vir] = left_ref[i]
-        keep[...] = one_hot(iota((aux - cut, aux - cut), 0) == iota((aux - cut, aux - cut), 1))
+        own[...] = jnp.where(core_ref[0] == 0, flat[:half, :], flat[half:, :])
         sums[...] = some(CHUNK)
 
     @pl.when((k > 0) & (k < last))
@@ -127,9 +128,8 @@
         scratch_shapes=[
             pltpu.VMEM((roots, ranks * share), jnp.float32),
             pltpu.VMEM((ranks * pitch, ranks * FIRST), jnp.bfloat16),
-            pltpu.VMEM((ranks * pitch, roots), jnp.bfloat16),
-            pltpu.VMEM((ranks * rest, ranks * rest), jnp.bfloat16),
             pltpu.VMEM((roots, steps * CHUNK), jnp.bfloat16),
+            pltpu.VMEM((roots // 2, steps * CHUNK), jnp.bfloat16),
         ],
         compiler_params=pltpu.CompilerParams(vmem_limit_bytes=HIGH),
     )(core, factors, lefts)

time: 156 us -> 155 us (level)
  no operation moved by 1% of the time
where the time goes in v5:
time: 155 us; the launch traced here: 154 us
  blocking collectives  60.4 us (39%)
  Pallas kernels  45.3 us (29%)
  starting transfers between devices  20 us (13%)
  waiting for transfers between devices  19.5 us (13%)
  matrix products  3.99 us (3%)
  local copies, waits for them, and re-layouts  3.59 us (2%)
    all_to_all x1, blocking collectives, exchange(): lax.all_to_all(blocks, 'pair', split_axis=0, concat_axis=0, tiled=True)  60.4 us
    pallas_call x1, Pallas kernels, slab_product(): pl.pallas_call(functools.partial(slab_kernel, dims), grid=(steps,), in_sp...  18 us
    all_to_all x2, waiting for transfers between devices, exchange(): lax.all_to_all(blocks, 'pair', split_axis=0, concat_axis=0, tiled=True)  14.1 us
    pallas_call x2, Pallas kernels, half_product(): pl.pallas_call(functools.partial(half_kernel, dims, place), in_specs=[VME...  12.3 us
    all_to_all x2, starting transfers between devices, exchange(): lax.all_to_all(blocks, 'pair', split_axis=0, concat_axis=0, tiled=True)  8.45 us
    pallas_call x1, Pallas kernels, pack(): pl.pallas_call(functools.partial(pack_kernel, dims), grid=(steps,), in_sp...  8.31 us
    dot_general x1, matrix products, body(): jnp.einsum('iap,rp->ria', chol_factors, coul_vec, preferred_element_type=...  3.99 us
    ppermute x1, starting transfers between devices, body(): got = lax.ppermute(give, 'chol', CORE_SWAP)  3.4 us
  transfers between devices with their start and end apart: 7, of which 5 were waited for; matrix products, arithmetic and copies ran while one was open for 3% of the time, Pallas kernels for 16%

profile of v5, /device:TPU:1, one launch (start us, length us, event | category | flops | bytes accessed | tf_op | source)
XLA Modules:
  0.0 154.4 jit_solution(17120966103537885446)
XLA Ops:
  0.0 0.0 copy-start.4
  0.0 0.9 copy-done.4
  0.9 8.3 %shard_map.46 = (bf16[512,4096]{1,0:T(8,128)(2,1)}, bf16[256,4096]{1,0:T(8,128)(2,1)S(1)}) custom-call(s32[1]{0:T(128)} %bitcast.core_ref, bf16[4000,640]{1,0:T(8,128)(2,1)} %bitcast.28, bf16[5,8,800]{2,1,0:T(8,128)(2,1)S(1)} %bitcast.27), custom_call_target="tpu_custom_call" | custom-call | tf_op jit(solution)/shard_map/pallas_call | solution.py:112
  9.2 0.0 copy-start.1
  9.2 60.4 %all_to_all.15 = bf16[32,16,4096]{2,1,0:T(8,128)(2,1)} all-to-all(bf16[32,16,4096]{2,1,0:T(8,128)(2,1)} %bitcast.29), channel_id=1, replica_groups=mesh['pair'=32,'chol'=4] {'pair'}, dimensions={0} | all-to-all | bytes 8388608 | tf_op jit(solution)/shard_map/all_to_all | solution.py:27
  69.6 0.0 copy-done.1
  69.6 2.0 %shard_map.47 = bf16[256,4096]{1,0:T(8,128)(2,1)} custom-call(bf16[512,4096]{1,0:T(8,128)(2,1)} %bitcast.19, bf16[256,4096]{1,0:T(8,128)(2,1)} %copy-done.1), custom_call_target="tpu_custom_call", output_to_operand_aliasing={{}: (1, {})} | custom-call | tf_op jit(solution)/shard_map/pallas_call | solution.py:157
  71.5 4.0 %all-to-all-start.1 = ((bf16[32,8,4096]{2,1,0:T(8,128)(2,1)}), bf16[32,8,4096]{2,1,0:T(8,128)(2,1)S(1)}, u32[]{:S(2)}, u32[]{:S(2)}) async-start(bf16[32,8,4096]{2,1,0:T(8,128)(2,1)} %bitcast.22), calls=%async_computation.1 | async-start | bytes 4194304 | tf_op jit(solution)/shard_map/all_to_all | solution.py:27
  75.5 0.0 copy-start
  75.6 2.2 %copy-done = bf16[32,16,4096]{2,1,0:T(8,128)(2,1)S(1)} copy-done((bf16[32,16,4096]{2,1,0:T(8,128)(2,1)S(1)}, bf16[32,16,4096]{2,1,0:T(8,128)(2,1)}, u32[]{:S(2)}) %copy-start) | copy-done | bytes 4194328
  77.7 1.4 shard_map.48.mine_ref.refs_2_
  79.1 0.0 copy-start.2
  79.1 2.3 %collective-permute-start = (bf16[800,640]{1,0:T(8,128)(2,1)S(1)}, bf16[800,640]{1,0:T(8,128)(2,1)}, u32[]{:S(2)}, u32[]{:S(2)}) collective-permute-start(bf16[800,640]{1,0:T(8,128)(2,1)S(1)} %shard_map.48.mine_ref.refs_2_), channel_id=1, source_target_pairs={{0,1},{1,0},{2,3},{3,2},{4,5},{5,4},{6,7},{7,6},{8,9},{9,8},{10,11... | collective-permute-start | bytes 3072008 | tf_op jit(solution)/shard_map/ppermute | solution.py:405
  81.5 2.4 %collective-permute-done.other_ref.refs_1_ = bf16[800,640]{1,0:T(8,128)(2,1)} collective-permute-done((bf16[800,640]{1,0:T(8,128)(2,1)S(1)}, bf16[800,640]{1,0:T(8,128)(2,1)}, u32[]{:S(2)}, u32[]{:S(2)}) %collective-permute-start) | collective-permute-done | bytes 1024032 | tf_op jit(solution)/shard_map/ppermute | solution.py:405
  83.8 0.0 copy-done.2
  83.8 18.0 %shard_map.49.refs_2_.refs_3_ = f32[1280,896]{1,0:T(8,128)} custom-call(bf16[512,4096]{1,0:T(8,128)(2,1)} %bitcast.20, bf16[800,640]{1,0:T(8,128)(2,1)} %copy-done.2, bf16[800,640]{1,0:T(8,128)(2,1)} %collective-permute-done.other_ref.refs_1_), custom_call_target="tpu_custom_call" | custom-call | flops 7864320000 | bytes 11264000 | tf_op jit(solution)/shard_map/pallas_call | solution.py:289
  101.9 0.9 all-to-all-done.1
  102.8 0.0 slice-start
  102.8 7.1 %shard_map.50 = (f32[7,640,128]{2,1,0:T(8,128)S(1)}, bf16[1280,800]{1,0:T(8,128)(2,1)S(1)}, bf16[1280,800]{1,0:T(8,128)(2,1)S(1)}) custom-call(bf16[256,4096]{1,0:T(8,128)(2,1)S(1)} %bitcast.25, bf16[800,640]{1,0:T(8,128)(2,1)} %collective-permute-done.other_ref.refs_1_, f32[1280,896]{1,0:T(8,128)} %shard_map.49.refs_2_.refs_3_), custom_call_target="tpu_custom_call" | custom-call | flops 2621440000 | bytes 6144000 | tf_op jit(solution)/shard_map/pallas_call | solution.py:337
  109.9 3.4 %collective-permute-start.1 = (f32[7,640,128]{2,1,0:T(8,128)S(1)}, f32[7,640,128]{2,1,0:T(8,128)S(1)}, u32[]{:S(2)}, u32[]{:S(2)}) collective-permute-start(f32[7,640,128]{2,1,0:T(8,128)S(1)} %get-tuple-element.16), channel_id=1, source_target_pairs={{0,1},{1,0},{2,3},{3,2},{4,5},{5,4},{6,7},{7,6},{8,9},{9,8},{10,11... | collective-permute-start | bytes 6881288 | tf_op jit(solution)/shard_map/ppermute | solution.py:410
  113.3 0.0 slice-done
  113.3 0.0 slice-done.1
  113.3 0.0 copy-done.3
  113.3 5.2 %shard_map.51.keep_ref = f32[7,640,128]{2,1,0:T(8,128)S(1)} custom-call(bf16[1280,800]{1,0:T(8,128)(2,1)S(1)} %get-tuple-element.14.refs_0_, bf16[1280,800]{1,0:T(8,128)(2,1)S(1)} %get-tuple-element.15.refs_1_, bf16[800,640]{1,0:T(8,128)(2,1)S(1)} %copy-done.3, f32[1280,896]{1,0:T(8,128)S(1)} %bitcast.24), custom_call_target="tpu_custom_call" | custom-call | flops 2621440000 | bytes 6144000 | tf_op jit(solution)/shard_map/pallas_call | solution.py:337
  118.5 0.0 collective-permute-done.1.other_ref
  118.5 3.3 %shard_map.52 = bf16[32,5,4,800]{3,2,1,0:T(4,128)(2,1)} custom-call(f32[7,640,128]{2,1,0:T(8,128)S(1)} %shard_map.51.keep_ref, f32[7,640,128]{2,1,0:T(8,128)S(1)} %collective-permute-done.1.other_ref), custom_call_target="tpu_custom_call" | custom-call | tf_op jit(solution)/shard_map/pallas_call | solution.py:372
  121.9 4.4 %all-to-all-start.2 = ((bf16[32,5,4,800]{3,2,1,0:T(4,128)(2,1)}), bf16[32,5,4,800]{3,2,1,0:T(4,128)(2,1)S(1)}, u32[]{:S(2)}, u32[]{:S(2)}) async-start(bf16[32,5,4,800]{3,2,1,0:T(4,128)(2,1)} %shard_map.52), calls=%async_computation.2 | async-start | bytes 2293760 | tf_op jit(solution)/shard_map/all_to_all | solution.py:27
  126.3 0.1 slice_bitcast_fusion
  126.4 0.1 slice.13
  126.5 0.1 reshape.67
  126.7 0.1 reshape.66
  126.8 0.0 copy-start.6
  126.8 0.0 copy-start.7
  126.8 0.0 copy-start.5
  126.8 4.0 %fusion.1 = f32[8,5,800]{2,0,1:T(8,128)S(1)} fusion(bf16[5,800,640]{2,1,0:T(8,128)(2,1)} %param.5, bf16[8,256]{1,0:T(8,128)(2,1)S(1)} %reshape.67, bf16[8,384]{1,0:T(8,128)(2,1)S(1)} %reshape.66), kind=kOutput, calls=%fused_computation.8 | convolution fusion | flops 40980480 | bytes 5258240 | tf_op jit(solution)/shard_map/iap,rp->ria/dot_general | solution.py:426
  130.9 0.5 collective-permute-start.2
  131.4 13.2 %all-to-all-done.2 = bf16[32,5,4,800]{3,2,1,0:T(4,128)(2,1)S(1)} async-done(((bf16[32,5,4,800]{3,2,1,0:T(4,128)(2,1)}), bf16[32,5,4,800]{3,2,1,0:T(4,128)(2,1)S(1)}, u32[]{:S(2)}, u32[]{:S(2)}) %all-to-all-start.2) | async-done | bytes 1024032 | tf_op jit(solution)/shard_map/all_to_all | solution.py:27
  144.6 0.5 convert_reduce_fusion
  145.1 0.0 collective-permute-done.2
  145.1 2.6 %collective-permute-start.3 = (f32[4,5,800]{2,0,1:T(4,128)S(1)}, f32[4,5,800]{2,0,1:T(4,128)S(1)}, u32[]{:S(2)}, u32[]{:S(2)}) collective-permute-start(f32[4,5,800]{2,0,1:T(4,128)S(1)} %bitcast_subtract_fusion), channel_id=1, source_target_pairs={{0,2},{2,0},{1,3},{3,1},{4,6},{6,4},{5,7},{7,5},{8,10},{10,8},{9,1... | collective-permute-start | bytes 192008 | tf_op jit(solution)/shard_map/ppermute | solution.py:432
  147.7 2.2 %collective-permute-done.3 = f32[4,5,800]{2,0,1:T(4,128)S(1)} collective-permute-done((f32[4,5,800]{2,0,1:T(4,128)S(1)}, f32[4,5,800]{2,0,1:T(4,128)S(1)}, u32[]{:S(2)}, u32[]{:S(2)}) %collective-permute-start.3) | collective-permute-done | bytes 64032 | tf_op jit(solution)/shard_map/ppermute | solution.py:432
  149.9 2.8 %collective-permute-start.4 = (f32[4,5,800]{2,0,1:T(4,128)S(1)}, f32[4,5,800]{2,0,1:T(4,128)S(1)}, u32[]{:S(2)}, u32[]{:S(2)}) collective-permute-start(f32[4,5,800]{2,0,1:T(4,128)S(1)} %add.18), channel_id=1, source_target_pairs={{0,1},{1,0},{2,3},{3,2},{4,5},{5,4},{6,7},{7,6},{8,9},{9,8},{10,11... | collective-permute-start | bytes 192008 | tf_op jit(solution)/shard_map/ppermute | solution.py:433
  152.7 0.0 copy-done.6
  152.7 0.0 copy-done.7
  152.7 0.1 broadcast_subtract_fusion
  152.8 0.8 collective-permute-done.4
  153.6 0.0 copy-done.5
  153.6 0.7 fusion
  (7 shorter events, 0.1 us)
Async XLA Ops:
  0.0 0.9 copy-start.4
  9.2 60.4 %copy-start.1 = (bf16[256,4096]{1,0:T(8,128)(2,1)}, bf16[256,4096]{1,0:T(8,128)(2,1)S(1)}, u32[]{:S(2)}) copy-start(bf16[256,4096]{1,0:T(8,128)(2,1)S(1)} %get-tuple-element.13.send_ref) | copy-start | bytes 6291460
  71.5 31.2 %all-to-all-start.1 = ((bf16[32,8,4096]{2,1,0:T(8,128)(2,1)}), bf16[32,8,4096]{2,1,0:T(8,128)(2,1)S(1)}, u32[]{:S(2)}, u32[]{:S(2)}) async-start(bf16[32,8,4096]{2,1,0:T(8,128)(2,1)} %bitcast.22), calls=%async_computation.1 | async-start | bytes 4194304 | tf_op jit(solution)/shard_map/all_to_all | solution.py:27
  75.5 2.2 %copy-start = (bf16[32,16,4096]{2,1,0:T(8,128)(2,1)S(1)}, bf16[32,16,4096]{2,1,0:T(8,128)(2,1)}, u32[]{:S(2)}) copy-start(bf16[32,16,4096]{2,1,0:T(8,128)(2,1)} %all_to_all.15) | copy-start | bytes 12582916
  79.1 4.7 %copy-start.2 = (bf16[800,640]{1,0:T(8,128)(2,1)}, bf16[800,640]{1,0:T(8,128)(2,1)S(1)}, u32[]{:S(2)}) copy-start(bf16[800,640]{1,0:T(8,128)(2,1)S(1)} %shard_map.48.mine_ref.refs_2_) | copy-start | bytes 3072004
  79.1 4.7 %collective-permute-start = (bf16[800,640]{1,0:T(8,128)(2,1)S(1)}, bf16[800,640]{1,0:T(8,128)(2,1)}, u32[]{:S(2)}, u32[]{:S(2)}) collective-permute-start(bf16[800,640]{1,0:T(8,128)(2,1)S(1)} %shard_map.48.mine_ref.refs_2_), channel_id=1, source_target_pairs={{0,1},{1,0},{2,3},{3,2},{4,5},{5,4},{6,7},{7,6},{8,9},{9,8},{10,11... | collective-permute-start | bytes 3072008 | tf_op jit(solution)/shard_map/ppermute | solution.py:405
  102.8 10.5 %slice-start = ((s8[4587520]{0:T(1024)(128)(4,1)}), s8[4194304]{0:T(1024)(128)(4,1)S(1)}, s32[]{:S(2)}) async-start(s8[4587520]{0:T(1024)(128)(4,1)} %bitcast.23), calls=%async_computation.3 | async-start | bytes 8388608
  102.8 10.5 %slice-start.1 = ((s8[4587520]{0:T(1024)(128)(4,1)}), s8[393216]{0:T(1024)(128)(4,1)S(1)}, s32[]{:S(2)}) async-start(s8[4587520]{0:T(1024)(128)(4,1)} %bitcast.23), calls=%async_computation.4 | async-start | bytes 786432
  102.8 10.5 %copy-start.3 = (bf16[800,640]{1,0:T(8,128)(2,1)S(1)}, bf16[800,640]{1,0:T(8,128)(2,1)}, u32[]{:S(2)}) copy-start(bf16[800,640]{1,0:T(8,128)(2,1)} %copy-done.2) | copy-start | bytes 3072004
  109.9 8.7 %collective-permute-start.1 = (f32[7,640,128]{2,1,0:T(8,128)S(1)}, f32[7,640,128]{2,1,0:T(8,128)S(1)}, u32[]{:S(2)}, u32[]{:S(2)}) collective-permute-start(f32[7,640,128]{2,1,0:T(8,128)S(1)} %get-tuple-element.16), channel_id=1, source_target_pairs={{0,1},{1,0},{2,3},{3,2},{4,5},{5,4},{6,7},{7,6},{8,9},{9,8},{10,11... | collective-permute-start | bytes 6881288 | tf_op jit(solution)/shard_map/ppermute | solution.py:410
  121.9 22.7 %all-to-all-start.2 = ((bf16[32,5,4,800]{3,2,1,0:T(4,128)(2,1)}), bf16[32,5,4,800]{3,2,1,0:T(4,128)(2,1)S(1)}, u32[]{:S(2)}, u32[]{:S(2)}) async-start(bf16[32,5,4,800]{3,2,1,0:T(4,128)(2,1)} %shard_map.52), calls=%async_computation.2 | async-start | bytes 2293760 | tf_op jit(solution)/shard_map/all_to_all | solution.py:27
  126.8 25.9 %copy-start.6 = (f32[800]{0:T(1024)S(1)}, f32[800]{0:T(1024)}, u32[]{:S(2)}) copy-start(f32[800]{0:T(1024)} %param.7) | copy-start | bytes 9604
  126.8 25.9 %copy-start.7 = (f32[5]{0:T(128)S(1)}, f32[5]{0:T(128)}, u32[]{:S(2)}) copy-start(f32[5]{0:T(128)} %param.6) | copy-start | bytes 64
  126.8 26.8 %copy-start.5 = (bf16[8,5,800]{2,0,1:T(8,128)(2,1)S(1)}, bf16[8,5,800]{2,0,1:T(8,128)(2,1)}, u32[]{:S(2)}) copy-start(bf16[8,5,800]{2,0,1:T(8,128)(2,1)} %param.4) | copy-start | bytes 192004
  130.9 14.2 %collective-permute-start.2 = (f32[4,5,800]{2,0,1:T(4,128)S(1)}, f32[4,5,800]{2,0,1:T(4,128)S(1)}, u32[]{:S(2)}, u32[]{:S(2)}) collective-permute-start(f32[4,5,800]{2,0,1:T(4,128)S(1)} %constant_dynamic-slice_fusion), channel_id=1, source_target_pairs={{0,1},{1,0},{2,3},{3,2},{4,5},{5,4},{6,7},{7,6},{8,9},{9,8},{10,11... | collective-permute-start | bytes 192008 | tf_op jit(solution)/shard_map/ppermute | solution.py:429
  145.1 4.8 %collective-permute-start.3 = (f32[4,5,800]{2,0,1:T(4,128)S(1)}, f32[4,5,800]{2,0,1:T(4,128)S(1)}, u32[]{:S(2)}, u32[]{:S(2)}) collective-permute-start(f32[4,5,800]{2,0,1:T(4,128)S(1)} %bitcast_subtract_fusion), channel_id=1, source_target_pairs={{0,2},{2,0},{1,3},{3,1},{4,6},{6,4},{5,7},{7,5},{8,10},{10,8},{9,1... | collective-permute-start | bytes 192008 | tf_op jit(solution)/shard_map/ppermute | solution.py:432
  149.9 3.7 %collective-permute-start.4 = (f32[4,5,800]{2,0,1:T(4,128)S(1)}, f32[4,5,800]{2,0,1:T(4,128)S(1)}, u32[]{:S(2)}, u32[]{:S(2)}) collective-permute-start(f32[4,5,800]{2,0,1:T(4,128)S(1)} %add.18), channel_id=1, source_target_pairs={{0,1},{1,0},{2,3},{3,2},{4,5},{5,4},{6,7},{7,6},{8,9},{9,8},{10,11... | collective-permute-start | bytes 192008 | tf_op jit(solution)/shard_map/ppermute | solution.py:433
